TPU v7x, 256 devices: a whole 4x4x8 slice. The times are simulated.
256 devices in a mesh: strip: 64 (over y, z_lo, x), group: 4 (over z_hi, core).
Axes of the slice: x: 4, y: 4, z: 8 (z_hi: 2, z_lo: 4; z = z_hi * 4 + z_lo), core: 2. Of those that a mesh axis runs over, the one named last changes fastest.
Arguments:
- initial: float32 [64, 256, 128], P('group', 'strip'), may hold values from -1 to 1
- react_rates: float32 [64], P('group'), may hold values from 0.02 to 0.1
- snap_times: int32 [64, 4], replicated, may hold values from 1 to 2
- field_code: bfloat16 [64, 512], replicated, may hold values from -6 to 6
- time_code: bfloat16 [2, 512], replicated, may hold values from -6 to 6
- batch_ids: int32 [2, 512], P(None, 'group'), may hold values from 0 to 63
- in_weight: bfloat16 [512, 512], replicated, may hold values from -0.25 to 0.25
- in_moment: float32 [512, 512], P('strip'), may hold values from -0.75 to 0.75
- in_second: float32 [512, 512], P('strip'), may hold values from 0.001 to 0.1
- out_weight: bfloat16 [512, 32768], P(None, 'strip'), may hold values from -0.75 to 0.75
- out_moment: float32 [512, 32768], P('group', 'strip'), may hold values from -0.0625 to 0.0625
- out_second: float32 [512, 32768], P('group', 'strip'), may hold values from 1e-06 to 0.0001
Outputs:
- fields_out: float32 [64, 256, 128], P('group', 'strip')
- in_weight_new: bfloat16 [512, 512], replicated
- in_moment_new: float32 [512, 512], P('strip')
- in_second_new: float32 [512, 512], P('strip')
- out_weight_new: bfloat16 [512, 32768], P(None, 'strip')
- out_moment_new: float32 [512, 32768], P('group', 'strip')
- out_second_new: float32 [512, 32768], P('group', 'strip')
Inputs may be any that keep to these rules, and one draw needn't show every extreme that they name: `snap_times`: the number of solver steps after which snapshot slot k of field f is taken. `batch_ids`: column c of a row names a sample of batch part c // 128: field id, slot c // 128.
All inputs are finite; a program needn't handle non-finite values.
Results may differ from a plain program's by a relative error of at most 0.001.
The roundings to bfloat16 on the way count: a program that leaves them out, or rounds other values in their place, can miss the bound.
Values may be sent and summed in bfloat16 or wider, within the bound.
A program may use at most 64 MiB of HBM per device.

v0:
```python
import jax
import jax.numpy as jnp
from jax import lax
from jax.sharding import PartitionSpec as P

STEPS = 2
SNAPS = 4
ADAM = 2
PRIOR = 100


DIFF_ROWS = 0.35
DIFF_COLS = 0.05
BETA_ONE = 0.9
BETA_TWO = 0.999
LEARN_RATE = 0.003
EPSILON = 1e-08
GELU_SCALE = 0.7978845608
GELU_CUBE = 0.044715


def extended(value, sides, width):
    for axis, dim in sides:
        peers, length = (lax.axis_size(axis), value.shape[dim])
        up = [(i, (i + 1) % peers) for i in range(peers - 1)]
        down = [(j, i) for i, j in up]
        last = lax.slice_in_dim(value, length - width, length, axis=dim)
        initial = lax.slice_in_dim(value, 0, width, axis=dim)
        before = lax.ppermute(last, axis, up)
        after = lax.ppermute(initial, axis, down)
        value = jnp.concatenate([before, value, after], axis=dim)
    return value


def advance(padded, react_rates):
    center = padded[:, 1:-1]
    across = jnp.roll(center, 1, 2) + jnp.roll(center, -1, 2)
    return (
        center
        + DIFF_ROWS * (padded[:, :-2] + padded[:, 2:] - 2.0 * center)
        + DIFF_COLS * (across - 2.0 * center)
        + react_rates[:, None, None] * center * (1.0 - center * center)
    )


def gelu_value(pre_act):
    return (
        0.5
        * pre_act
        * (1.0 + jnp.tanh(GELU_SCALE * (pre_act + GELU_CUBE * pre_act * pre_act * pre_act)))
    )


def gelu_slope(pre_act):
    tanh_part = jnp.tanh(GELU_SCALE * (pre_act + GELU_CUBE * pre_act * pre_act * pre_act))
    return 0.5 * (1.0 + tanh_part) + 0.5 * pre_act * (1.0 - tanh_part * tanh_part) * GELU_SCALE * (
        1.0 + 3.0 * GELU_CUBE * pre_act * pre_act
    )


def adam_update(weight, moment, second, gradient, step_count):
    moment = BETA_ONE * moment + (1.0 - BETA_ONE) * gradient
    second = BETA_TWO * second + (1.0 - BETA_TWO) * gradient * gradient
    update = (
        moment
        / (1.0 - BETA_ONE**step_count)
        / (jnp.sqrt(second / (1.0 - BETA_TWO**step_count)) + EPSILON)
    )
    return ((weight.astype(jnp.float32) - LEARN_RATE * update).astype(jnp.bfloat16), moment, second)


def keep_snapshot(snapshots, own_times, field_state, solver_step):
    chosen = (own_times == solver_step + 1)[:, :, None, None]
    return jnp.where(chosen, field_state.astype(jnp.bfloat16)[:, None], snapshots)


def shards(
    initial,
    react_rates,
    snap_times,
    field_code,
    time_code,
    batch_ids,
    in_weight,
    in_moment,
    in_second,
    out_weight,
    out_moment,
    out_second,
):
    strip_index = lax.axis_index("strip")
    group_index = lax.axis_index("group")
    strips = lax.axis_size("strip")
    groups = lax.axis_size("group")
    fields_dev = initial.shape[0]
    rows_dev = initial.shape[1]
    columns = initial.shape[2]
    own_times = lax.dynamic_slice_in_dim(snap_times, group_index * fields_dev, fields_dev, 0)
    snapshots = jnp.zeros((fields_dev, SNAPS, rows_dev, columns), jnp.bfloat16)
    field_state = initial
    for solver_step in range(STEPS):
        padded = extended(field_state, (("strip", 1),), 1)
        field_state = advance(padded, react_rates)
        snapshots = keep_snapshot(snapshots, own_times, field_state, solver_step)
    points_dev = rows_dev * columns
    piece_len = points_dev // strips
    snap_part = SNAPS // groups
    flat_snaps = snapshots.reshape(fields_dev, SNAPS, strips, piece_len)
    outgoing = jnp.transpose(flat_snaps, (2, 1, 3, 0)).reshape(
        strips, SNAPS, piece_len * fields_dev
    )
    arrived = lax.all_to_all(
        lax.all_to_all(outgoing, "strip", split_axis=0, concat_axis=0, tiled=True),
        "group",
        split_axis=1,
        concat_axis=2,
        tiled=True,
    )
    arrived = arrived.reshape(strips, snap_part, groups, piece_len, fields_dev)
    sample_pool = jnp.transpose(arrived, (2, 4, 1, 0, 3)).reshape(
        groups * fields_dev * snap_part, points_dev
    )
    batch_rows = batch_ids.shape[1]
    total_batch = batch_rows * groups
    hidden_width = in_weight.shape[0]
    in_rows = hidden_width // strips
    out_rows = hidden_width // groups
    field_count = field_code.shape[0]
    flat_times = snap_times.reshape(-1)
    pool_size = sample_pool.shape[0]
    for adam_turn in range(ADAM):
        sample_ids = batch_ids[adam_turn]
        field_of = sample_ids // snap_part
        slot_of = group_index * snap_part + sample_ids % snap_part
        time_match = (field_of * SNAPS + slot_of)[:, None] == jnp.arange(
            field_count * SNAPS, dtype=jnp.int32
        )[None, :]
        time_of = jnp.sum(jnp.where(time_match, flat_times[None, :], 0), axis=1)
        pick_field = (
            field_of[:, None] == jnp.arange(field_count, dtype=jnp.int32)[None, :]
        ).astype(jnp.bfloat16)
        pick_time = ((time_of - 1)[:, None] == jnp.arange(STEPS, dtype=jnp.int32)[None, :]).astype(
            jnp.bfloat16
        )
        inputs = (
            jnp.dot(pick_field, field_code, preferred_element_type=jnp.float32)
            + jnp.dot(pick_time, time_code, preferred_element_type=jnp.float32)
        ).astype(jnp.bfloat16)
        pick_pool = (sample_ids[:, None] == jnp.arange(pool_size, dtype=jnp.int32)[None, :]).astype(
            jnp.bfloat16
        )
        target = jnp.dot(pick_pool, sample_pool, preferred_element_type=jnp.float32)
        pre_act = lax.dot_general(
            inputs, in_weight, (((1,), (1,)), ((), ())), preferred_element_type=jnp.float32
        )
        hidden = gelu_value(pre_act).astype(jnp.bfloat16)
        predict = jnp.dot(hidden, out_weight, preferred_element_type=jnp.float32)
        delta_out = ((predict - target) / total_batch).astype(jnp.bfloat16)
        out_grad = lax.psum_scatter(
            lax.dot_general(
                hidden, delta_out, (((0,), (0,)), ((), ())), preferred_element_type=jnp.float32
            ),
            "group",
            scatter_dimension=0,
            tiled=True,
        )
        weight_rows = out_weight
        hidden_grad = lax.psum_scatter(
            lax.dot_general(
                weight_rows, delta_out, (((1,), (1,)), ((), ())), preferred_element_type=jnp.float32
            ),
            "strip",
            scatter_dimension=0,
            tiled=True,
        )
        own_pre = jnp.transpose(
            lax.dynamic_slice_in_dim(pre_act, strip_index * in_rows, in_rows, 1)
        )
        pre_grad = (hidden_grad * gelu_slope(own_pre)).astype(jnp.bfloat16)
        in_grad = lax.psum(jnp.dot(pre_grad, inputs, preferred_element_type=jnp.float32), "group")
        step_count = PRIOR + adam_turn + 1
        own_in = lax.dynamic_slice_in_dim(in_weight, strip_index * in_rows, in_rows, 0)
        new_in, in_moment, in_second = adam_update(
            own_in, in_moment, in_second, in_grad, step_count
        )
        own_out = lax.dynamic_slice_in_dim(out_weight, group_index * out_rows, out_rows, 0)
        new_out, out_moment, out_second = adam_update(
            own_out, out_moment, out_second, out_grad, step_count
        )
        in_weight = lax.all_gather(new_in, "strip", axis=0, tiled=True)
        out_weight = lax.all_gather(new_out, "group", axis=0, tiled=True)
    return (field_state, in_weight, in_moment, in_second, out_weight, out_moment, out_second)


def solution(mesh):
    in_specs = (
        P("group", "strip", None),
        P("group"),
        P(),
        P(),
        P(),
        P(None, "group"),
        P(),
        P("strip", None),
        P("strip", None),
        P(None, "strip"),
        P("group", "strip"),
        P("group", "strip"),
    )
    out_specs = (
        P("group", "strip", None),
        P(),
        P("strip", None),
        P("strip", None),
        P(None, "strip"),
        P("group", "strip"),
        P("group", "strip"),
    )
    return jax.shard_map(shards, mesh=mesh, in_specs=in_specs, out_specs=out_specs, check_vma=False)
```

profile of v0, /device:TPU:1, one launch (start us, length us, event | category | flops | bytes accessed | tf_op | source)
XLA Modules:
  0.0 1842.3 jit_solution(2729489665720516930)
XLA Ops:
  8.0 0.9 fusion.103
  8.9 3.9 collective-permute-start
  12.9 1.3 collective-permute-start.1
  14.3 0.7 copy-done.11
  15.0 0.7 copy-done.10
  15.7 0.1 copy.47
  15.8 0.1 broadcast_in_dim.91
  15.9 0.2 select_reduce_fusion.1
  16.1 0.2 fusion.19
  16.4 0.4 copy-done.9
  16.8 0.2 fusion.4
  17.1 0.1 broadcast_in_dim.96
  17.2 0.1 broadcast_in_dim.104
  17.4 0.6 copy-done.12
  18.0 0.1 fusion.98
  18.2 4.0 collective-permute-start.2
  22.2 1.3 collective-permute-start.3
  23.6 0.1 copy.51
  23.8 0.1 copy.52
  24.0 2.6 collective-permute-done.3
  26.6 0.7 fusion.96
  27.4 0.1 copy.48
  27.5 0.1 copy.49
  27.7 0.7 select_select_fusion
  28.4 19.9 %all-to-all-start = ((bf16[64,4,128]{2,1,0:T(4,128)(2,1)}), bf16[64,4,128]{2,1,0:T(4,128)(2,1)S(1)}, u32[]{:S(2)}, u32[]{:S(2)}) async-start(bf16[64,4,128]{2,1,0:T(4,128)(2,1)} %select_select_fusion), calls=%async_computation | async-start | bytes 131072 | tf_op jit(solution)/shard_map/all_to_all | solution.py:113
  48.3 0.3 fusion.106
  48.6 8.7 all-to-all-done
  57.4 0.6 copy.54
  58.0 12.1 all-to-all-start.1
  70.1 0.3 fusion.92
  70.4 6.9 all-to-all-done.1
  77.3 0.1 copy.55
  77.4 0.8 copy.56
  78.2 0.3 reshape.69
  78.5 0.2 fusion.2
  78.7 1.0 convolution_bitcast_fusion
  79.8 1.3 fusion.90
  81.4 0.7 copy-done.13
  82.1 0.6 dynamic-slice
  83.3 0.2 fusion.18
  83.6 0.2 fusion.5
  83.8 625.2 %all-reduce.5.cloned.1.call-done = f32[512,128]{0,1:T(8,128)} async-done(((f32[512,128]{0,1:T(8,128)}), f32[512,128]{0,1:T(8,128)}) %all-reduce.5.cloned.1.call-update) | async-done | bytes 262160
  709.0 0.9 constant_dynamic-slice_fusion.4
  710.0 0.2 fusion.64
  710.1 44.9 %psum.14 = f32[8,512]{1,0:T(8,128)S(1)} all-reduce(f32[8,512]{1,0:T(8,128)S(1)} %fusion.64), channel_id=1, replica_groups=mesh['strip'=64,'group'=4] {'group'}, use_global_device_ids=true, to_apply=%region_2.3 | all-reduce | flops 4096 | bytes 32768 | tf_op jit(solution)/shard_map/psum | solution.py:180
  755.1 157.3 %all_gather.12 = bf16[512,512]{1,0:T(8,128)(2,1)S(1)} all-gather(bf16[8,512]{1,0:T(8,128)(2,1)S(1)} %subtract_convert_fusion.3), channel_id=1, replica_groups=mesh['strip'=64,'group'=4] {'strip'}, dimensions={0}, use_global_device_ids=true | all-gather | bytes 532480 | tf_op jit(solution)/shard_map/all_gather | solution.py:190
  912.4 0.3 fusion.107
  912.8 0.6 copy-done.2
  913.5 1.1 subtract_convert_fusion.1
  914.6 40.3 %all_gather.13 = bf16[512,512]{1,0:T(8,128)(2,1)S(1)} all-gather(bf16[128,512]{1,0:T(8,128)(2,1)S(1)} %subtract_convert_fusion.1), channel_id=1, replica_groups=mesh['strip'=64,'group'=4] {'group'}, dimensions={0}, use_global_device_ids=true | all-gather | bytes 655360 | tf_op jit(solution)/shard_map/all_gather | solution.py:191
  954.9 0.2 fusion.88
  955.1 0.2 fusion.3
  955.4 1.0 fusion.108
  956.5 1.3 fusion.86
  958.0 629.3 %all-reduce.7.cloned.1.call-done = f32[512,128]{0,1:T(8,128)} async-done(((f32[512,128]{0,1:T(8,128)}), f32[512,128]{0,1:T(8,128)}) %all-reduce.7.cloned.1.call-update) | async-done | bytes 262160
  1587.3 0.9 constant_dynamic-slice_fusion.3
  1588.3 0.2 fusion.62
  1588.4 44.8 %psum.15 = f32[8,512]{1,0:T(8,128)S(1)} all-reduce(f32[8,512]{1,0:T(8,128)S(1)} %fusion.62), channel_id=1, replica_groups=mesh['strip'=64,'group'=4] {'group'}, use_global_device_ids=true, to_apply=%region_6.7 | all-reduce | flops 4096 | bytes 32768 | tf_op jit(solution)/shard_map/psum | solution.py:180
  1633.2 0.6 subtract_convert_fusion.2
  1633.8 157.4 %all_gather.14 = bf16[512,512]{1,0:T(8,128)(2,1)S(1)} all-gather(bf16[8,512]{1,0:T(8,128)(2,1)S(1)} %get-tuple-element.12), channel_id=1, replica_groups=mesh['strip'=64,'group'=4] {'strip'}, dimensions={0}, use_global_device_ids=true | all-gather | bytes 532480 | tf_op jit(solution)/shard_map/all_gather | solution.py:190
  1791.3 2.0 subtract_convert_fusion
  1793.3 40.0 %all_gather.15 = bf16[512,512]{1,0:T(8,128)(2,1)S(1)} all-gather(bf16[128,512]{1,0:T(8,128)(2,1)S(1)} %get-tuple-element.9), channel_id=1, replica_groups=mesh['strip'=64,'group'=4] {'group'}, dimensions={0}, use_global_device_ids=true | all-gather | bytes 655360 | tf_op jit(solution)/shard_map/all_gather | solution.py:191
  1833.3 0.8 copy.73
  1834.1 0.8 copy.74
  (56 shorter events, 1.4 us)
Async XLA Ops:
  8.0 8.1 copy-start
  8.0 6.1 copy-start.5
  8.9 8.4 collective-permute-start
  12.9 4.5 collective-permute-start.1
  14.3 0.7 copy-start.11
  15.0 0.7 copy-start.10
  16.1 0.7 copy-start.9
  17.3 0.7 copy-start.12
  18.2 5.8 collective-permute-start.2
  22.2 4.4 collective-permute-start.3
  23.7 24.6 %copy-start.6 = (bf16[512,512]{1,0:T(8,128)(2,1)S(1)}, bf16[512,512]{1,0:T(8,128)(2,1)}, u32[]{:S(2)}) copy-start(bf16[512,512]{1,0:T(8,128)(2,1)} %param.18) | copy-start | bytes 1572868
  28.4 29.0 %all-to-all-start = ((bf16[64,4,128]{2,1,0:T(4,128)(2,1)}), bf16[64,4,128]{2,1,0:T(4,128)(2,1)S(1)}, u32[]{:S(2)}, u32[]{:S(2)}) async-start(bf16[64,4,128]{2,1,0:T(4,128)(2,1)} %select_select_fusion), calls=%async_computation | async-start | bytes 131072 | tf_op jit(solution)/shard_map/all_to_all | solution.py:113
  48.3 21.8 %copy-start.1 = (bf16[512,512]{1,0:T(8,128)(2,1)S(1)}, bf16[512,512]{1,0:T(8,128)(2,1)}, u32[]{:S(2)}) copy-start(bf16[512,512]{1,0:T(8,128)(2,1)} %param.21) | copy-start | bytes 1572868
  58.0 19.3 %all-to-all-start.1 = ((bf16[64,4,128]{2,0,1:T(8,128)(2,1)}), bf16[64,4,128]{2,0,1:T(8,128)(2,1)S(1)}, u32[]{:S(2)}, u32[]{:S(2)}) async-start(bf16[64,4,128]{2,0,1:T(8,128)(2,1)} %copy.54), calls=%async_computation.1 | async-start | bytes 131072 | tf_op jit(solution)/shard_map/all_to_all | solution.py:112
  70.1 638.9 %all-reduce.5.cloned.1.call-start = ((), (), s32[]{:S(2)}) async-start(), calls=%async_computation.6 | async-start | bytes 524288
  79.8 833.0 %reduce-scatter.5.cloned.1.call-start = ((), (), s32[]{:S(2)}) async-start(), calls=%async_computation.4 | async-start | bytes 1310720 | tf_op jit(solution)/shard_map/reduce_scatter | solution.py:159
  81.2 1506.1 %all-reduce.7.cloned.1.call-start = ((), (), s32[]{:S(2)}) async-start(), calls=%async_computation.7 | async-start | bytes 524288
  81.4 0.7 copy-start.13
  710.1 44.9 %copy-start.7 = (f32[8,512]{1,0:T(8,128)S(1)}, f32[8,512]{1,0:T(8,128)}, u32[]{:S(2)}) copy-start(f32[8,512]{1,0:T(8,128)} %param.19) | copy-start | bytes 49156
  710.1 44.9 %copy-start.8 = (f32[8,512]{1,0:T(8,128)S(1)}, f32[8,512]{1,0:T(8,128)}, u32[]{:S(2)}) copy-start(f32[8,512]{1,0:T(8,128)} %param.20) | copy-start | bytes 49156
  912.4 1.0 copy-start.2
  912.4 1.0 copy-start.3
  956.4 834.9 %reduce-scatter.7.cloned.1.call-start = ((), (), s32[]{:S(2)}) async-start(), calls=%async_computation.5 | async-start | bytes 1310720 | tf_op jit(solution)/shard_map/reduce_scatter | solution.py:159
  1633.8 157.5 %copy-start.4 = (f32[128,512]{1,0:T(8,128)S(1)}, f32[128,512]{1,0:T(8,128)}, u32[]{:S(2)}) copy-start(f32[128,512]{1,0:T(8,128)} %reduce-scatter.5.cloned.1.call-done) | copy-start | bytes 786436
Sparse Core Ops, SparseCore 0:
  79.9 629.0 all-reduce.4
  956.5 630.7 all-reduce.6
Sparse Core Ops, SparseCore 1:
  83.2 38.4 reduce-scatter.4
  959.9 40.0 reduce-scatter.6
where the time goes:
time: 1840 us
  waiting for transfers between devices  1270 us (69%)
  blocking collectives  485 us (26%)
  starting transfers between devices  42.6 us (2%)
    unnamed x6, waiting for transfers between devices  1250 us
    all_gather x2, blocking collectives, shards(): in_weight = lax.all_gather(new_in, 'strip', axis=0, tiled=True)  315 us
    psum x2, blocking collectives, shards(): lax.psum(jnp.dot(pre_grad, inputs, preferred_element_type=jnp.float32), '...  89.7 us
    all_gather x2, blocking collectives, shards(): out_weight = lax.all_gather(new_out, 'group', axis=0, tiled=True)  80.3 us
  transfers between devices with their start and end apart: 10, of which 5 were waited for; matrix products, arithmetic and copies ran while one was open for 1% of the time, Pallas kernels for 0%

commit v1 on v0

v1 whole, which is shorter than its diff:
```python
import functools

import jax
import jax.numpy as jnp
from jax import lax
from jax.experimental import pallas as pl
from jax.experimental.pallas import tpu as pltpu
from jax.sharding import PartitionSpec as P

STEPS = 2
SNAPS = 4
ADAM = 2
PRIOR = 100

DIFF_ROWS = 0.35
DIFF_COLS = 0.05
BETA_ONE = 0.9
BETA_TWO = 0.999
LEARN_RATE = 0.003
EPSILON = 1e-08
GELU_SCALE = 0.7978845608
GELU_CUBE = 0.044715

MESH = pl.DeviceIdType.MESH
F32 = jnp.float32
BF16 = jnp.bfloat16


def gelu_value(pre_act):
    return (
        0.5
        * pre_act
        * (1.0 + jnp.tanh(GELU_SCALE * (pre_act + GELU_CUBE * pre_act * pre_act * pre_act)))
    )


def gelu_slope(pre_act):
    tanh_part = jnp.tanh(GELU_SCALE * (pre_act + GELU_CUBE * pre_act * pre_act * pre_act))
    return 0.5 * (1.0 + tanh_part) + 0.5 * pre_act * (1.0 - tanh_part * tanh_part) * GELU_SCALE * (
        1.0 + 3.0 * GELU_CUBE * pre_act * pre_act
    )


def adam_update(weight, moment, second, gradient, step_count):
    moment = BETA_ONE * moment + (1.0 - BETA_ONE) * gradient
    second = BETA_TWO * second + (1.0 - BETA_TWO) * gradient * gradient
    update = (
        moment
        / (1.0 - BETA_ONE**step_count)
        / (jnp.sqrt(second / (1.0 - BETA_TWO**step_count)) + EPSILON)
    )
    return ((weight.astype(F32) - LEARN_RATE * update).astype(BF16), moment, second)


def dot(left, right, left_dim, right_dim):
    return lax.dot_general(
        left, right, (((left_dim,), (right_dim,)), ((), ())), preferred_element_type=F32
    )


def three_parts(value):
    high = value.astype(BF16)
    rest = value - high.astype(F32)
    middle = rest.astype(BF16)
    low = (rest - middle.astype(F32)).astype(BF16)
    return high, middle, low


def kernel(
    initial,
    rates,
    times,
    field_code,
    time_code,
    batch_ids,
    in_weight,
    in_moment,
    in_second,
    out_weight,
    out_moment,
    out_second,
    fields_out,
    in_weight_new,
    in_moment_new,
    in_second_new,
    out_weight_new,
    out_moment_new,
    out_second_new,
    edges,
    halo,
    states,
    pieces,
    from_own,
    from_far,
    half_pool,
    core_pool,
    counts,
    terms,
    term_in,
    hidden_own,
    hidden_all,
    rows_own,
    weight_mid,
    halo_send,
    halo_recv,
    piece_send,
    own_recv,
    far_recv,
    pool_send,
    pool_recv,
    count_send,
    count_recv,
    term_send,
    term_recv,
    hidden_send,
    hidden_recv,
    weight_send,
    weight_recv,
    row_send,
    row_recv,
):
    strips = lax.axis_size("strip")
    me = lax.axis_index("strip")
    g = lax.axis_index("group")
    far = lax.rem(g + 2, 4)
    mate = g + 1 - 2 * lax.rem(g, 2)
    far_mate = lax.rem(mate + 2, 4)
    fields = initial.shape[0]
    others = strips - 1

    def other(k):
        return lax.rem(me + 1 + k, strips)

    def send(source, target, send_sem, recv_sem, strip, group):
        copy = pltpu.make_async_remote_copy(
            src_ref=source,
            dst_ref=target,
            send_sem=send_sem,
            recv_sem=recv_sem,
            device_id={"strip": strip, "group": group},
            device_id_type=MESH,
        )
        copy.start()
        return copy

    barrier = pltpu.get_barrier_semaphore()

    def greet(strip, group):
        pl.semaphore_signal(
            barrier, inc=1, device_id={"strip": strip, "group": group}, device_id_type=MESH
        )

    def greet_strip(k, carry):
        greet(other(k), g)
        greet(other(k), far)
        return carry

    lax.fori_loop(0, others, greet_strip, 0)
    greet(me, far)
    greet(me, mate)
    greet(me, far_mate)

    edges[0] = initial[:, 0:2, :]
    edges[1] = initial[:, 2:4, :]

    kind_row = lax.broadcasted_iota(jnp.int32, (128, 128), 0)
    field_row = 16 * (kind_row // 32) + lax.rem(kind_row, 16)
    kind_lane = lax.broadcasted_iota(jnp.int32, (64, 128), 1)
    field_lane = 16 * (kind_lane // 32) + lax.rem(kind_lane, 16)
    spread = (lax.broadcasted_iota(jnp.int32, (64, 128), 0) == field_lane).astype(F32).astype(BF16)
    kind_times = dot(times[...].astype(F32).astype(BF16), spread, 1, 0)
    slot = lax.broadcasted_iota(jnp.int32, (4, 128), 0)
    own_time = jnp.sum(jnp.where(slot == g, kind_times, 0.0), axis=0, keepdims=True)
    step_lane = (lax.rem(lax.broadcasted_iota(jnp.int32, (1, 128), 1) // 16, 2) + 1).astype(F32)
    time_fits = jnp.where(own_time == step_lane, 1.0, 0.0)
    ones = jnp.ones((8, 128), BF16)
    for turn in range(ADAM):
        hits = (batch_ids[turn : turn + 1, :] == field_row).astype(F32).astype(BF16)
        counts[0, turn] = dot(ones, hits, 1, 1) * time_fits

    pl.semaphore_wait(barrier, 2 * others + 3)

    up = lax.rem(me + others, strips)
    down = lax.rem(me + 1, strips)
    halo_copies = [
        send(edges.at[0], halo.at[1], halo_send.at[0], halo_recv.at[1], up, g),
        send(edges.at[1], halo.at[0], halo_send.at[1], halo_recv.at[0], down, g),
    ]
    count_copies = [
        send(counts.at[0], counts.at[1 + i], count_send.at[i], count_recv.at[i], me, group)
        for i, group in enumerate((far, mate, far_mate))
    ]

    code_parts = []
    for part in range(4):
        for step in range(STEPS):
            code_parts.append(
                (
                    field_code[16 * part : 16 * part + 16, :].astype(F32)
                    + time_code[step : step + 1, :].astype(F32)
                ).astype(BF16)
            )
    code = jnp.concatenate(code_parts, axis=0)
    hidden_width = 8 * strips
    pre_act = dot(in_weight[...].reshape(hidden_width, 512), code, 1, 1)
    hidden = gelu_value(pre_act).astype(BF16)
    hidden_all[0] = hidden.reshape(strips, 8, 128)
    old_weight = out_weight[...].reshape(hidden_width, 512)
    predict = dot(hidden, old_weight, 0, 0)
    own_pre = dot(in_weight[me], code, 1, 1)

    for copy in halo_copies:
        copy.wait()

    row = lax.broadcasted_iota(jnp.int32, (8, 128), 0) + 4 * me - 2
    inside = jnp.logical_and(row >= 0, row < 4 * strips)

    def advance(center, rate):
        across = pltpu.roll(center, 1, 1) + pltpu.roll(center, 127, 1)
        return (
            center
            + DIFF_ROWS * (pltpu.roll(center, 1, 0) + pltpu.roll(center, 7, 0) - 2.0 * center)
            + DIFF_COLS * (across - 2.0 * center)
            + rate * center * (1.0 - center * center)
        )

    for field in range(fields):
        start = jnp.concatenate([halo[0, field], initial[field], halo[1, field]], axis=0)
        start = jnp.where(inside, start, 0.0)
        first = jnp.where(inside, advance(start, rates[field]), 0.0)
        second = advance(first, rates[field])
        states[8 * field : 8 * field + 8, :] = first
        states[8 * (fields + field) : 8 * (fields + field) + 8, :] = second
        fields_out[field] = second[2:6, :]

    place_row = lax.broadcasted_iota(jnp.int32, (32, 128), 0)
    place_lane = lax.broadcasted_iota(jnp.int32, (32, 128), 1)
    place = (place_lane == place_row + 32 * g).astype(F32).astype(BF16)
    for line in range(4):
        chosen = states[pl.ds(2 + line, 32, stride=8), :].astype(BF16)
        piece = dot(chosen, place, 0, 0).astype(BF16)
        pieces[16 * line : 16 * line + 16] = piece.reshape(16, 8, 128)

    def send_piece(k, carry):
        t = other(k)
        send(pieces.at[t], from_own.at[me], piece_send.at[0], own_recv.at[0], t, g)
        send(pieces.at[t], from_far.at[me], piece_send.at[1], far_recv.at[0], t, far)
        return carry

    lax.fori_loop(0, others, send_piece, 0)
    send(pieces.at[me], from_far.at[me], piece_send.at[1], far_recv.at[0], me, far)
    from_own[me] = pieces[me]

    def whole(source, target, send_sem, recv_sem):
        return pltpu.make_async_remote_copy(
            src_ref=source,
            dst_ref=target,
            send_sem=send_sem,
            recv_sem=recv_sem,
            device_id={"strip": me, "group": far},
            device_id_type=MESH,
        )

    most = pl.ds(0, others)
    own_all = whole(pieces.at[most], from_own.at[most], piece_send.at[0], own_recv.at[0])
    far_all = whole(pieces, from_far, piece_send.at[1], far_recv.at[0])
    own_all.wait_recv()
    far_all.wait_recv()
    half_pool[...] = from_own[...] + from_far[...]
    pool_copy = send(half_pool, core_pool, pool_send.at[0], pool_recv.at[0], me, mate)
    for copy in count_copies:
        copy.wait()
    count = jnp.sum(counts[...], axis=0)
    pool_copy.wait()
    pool = (half_pool[...] + core_pool[...]).reshape(8 * strips, 128).astype(F32).T

    moment, second_moment = out_moment[...], out_second[...]
    row_weight, row_moment, row_second = in_weight[me], in_moment[...], in_second[...]
    current = out_weight
    for turn in range(ADAM):
        step_count = PRIOR + turn + 1
        number = count[turn, 0:1, :]
        delta = ((predict - pool) * (1.0 / 512.0)).astype(BF16)
        terms[turn] = dot(current[...].reshape(hidden_width, 512), delta, 1, 1).reshape(
            strips, 8, 128
        )

        def send_terms(k, carry):
            t = other(k)
            send(
                terms.at[turn, t],
                term_in.at[turn, me],
                term_send.at[turn],
                term_recv.at[turn],
                t,
                g,
            )
            return carry

        lax.fori_loop(0, others, send_terms, 0)
        term_in[turn, me] = terms[turn, me]

        own_hidden = hidden_all[turn, pl.ds(g * (strips // 4), strips // 4)].reshape(
            hidden_width // 4, 128
        )
        grad = sum(dot(part, delta, 1, 0) for part in three_parts(own_hidden.astype(F32) * number))
        new_rows, moment, second_moment = adam_update(
            current[g], moment, second_moment, grad, step_count
        )
        following = weight_mid if turn + 1 < ADAM else out_weight_new
        following[g] = new_rows
        weight_copies = [
            send(
                following.at[g],
                following.at[g],
                weight_send.at[turn, i],
                weight_recv.at[turn, i],
                me,
                group,
            )
            for i, group in enumerate((far, mate))
        ]

        term_all = whole(
            terms.at[turn, most], term_in.at[turn, most], term_send.at[turn], term_recv.at[turn]
        )
        term_all.wait_recv()
        hidden_grad = jnp.sum(term_in[turn], axis=0)
        pre_grad = (hidden_grad * gelu_slope(own_pre)).astype(BF16)
        in_grad = sum(dot(part, code, 1, 0) for part in three_parts(pre_grad.astype(F32) * number))
        row_weight, row_moment, row_second = adam_update(
            row_weight, row_moment, row_second, in_grad, step_count
        )
        if turn + 1 < ADAM:
            own_pre = dot(row_weight, code, 1, 1)
            hidden_own[...] = gelu_value(own_pre).astype(BF16)
            source, gathered, send_sem, recv_sem = hidden_own, hidden_all.at[1], hidden_send, hidden_recv
            hidden_all[1, me] = hidden_own[...]
        else:
            rows_own[...] = row_weight
            source, gathered, send_sem, recv_sem = rows_own, in_weight_new, row_send, row_recv
            in_weight_new[me] = row_weight

        def send_rows(k, carry):
            t = other(k)
            send(source, gathered.at[me], send_sem.at[0], recv_sem.at[0], t, g)
            return carry

        lax.fori_loop(0, others, send_rows, 0)
        if turn + 1 == ADAM:
            in_moment_new[...] = row_moment
            in_second_new[...] = row_second
            out_moment_new[...] = moment
            out_second_new[...] = second_moment
        for copy in weight_copies:
            copy.wait()
        send(
            following.at[far],
            following.at[far],
            weight_send.at[turn, 2],
            weight_recv.at[turn, 2],
            me,
            mate,
        ).wait()
        rows_all = whole(gathered.at[most], gathered.at[most], send_sem.at[0], recv_sem.at[0])
        rows_all.wait()
        term_all.wait_send()
        if turn + 1 < ADAM:
            current = following
            predict = dot(
                hidden_all[1].reshape(hidden_width, 128),
                current[...].reshape(hidden_width, 512),
                0,
                0,
            )
    own_all.wait_send()
    far_all.wait_send()


def shards(
    initial,
    react_rates,
    snap_times,
    field_code,
    time_code,
    batch_ids,
    in_weight,
    in_moment,
    in_second,
    out_weight,
    out_moment,
    out_second,
):
    strips = lax.axis_size("strip")
    fields_dev = initial.shape[0]
    hidden_width = in_weight.shape[0]
    points = out_weight.shape[1]
    vmem = pl.BlockSpec(memory_space=pltpu.VMEM)
    smem = pl.BlockSpec(memory_space=pltpu.SMEM)
    dma = pltpu.SemaphoreType.DMA
    outs = pl.pallas_call(
        kernel,
        out_shape=(
            jax.ShapeDtypeStruct(initial.shape, F32),
            jax.ShapeDtypeStruct((strips, 8, in_weight.shape[1]), BF16),
            jax.ShapeDtypeStruct(in_moment.shape, F32),
            jax.ShapeDtypeStruct(in_second.shape, F32),
            jax.ShapeDtypeStruct((4, hidden_width // 4, points), BF16),
            jax.ShapeDtypeStruct(out_moment.shape, F32),
            jax.ShapeDtypeStruct(out_second.shape, F32),
        ),
        in_specs=[vmem, smem] + [vmem] * 10,
        out_specs=(vmem,) * 7,
        scratch_shapes=[
            pltpu.VMEM((2, fields_dev, 2, 128), F32),
            pltpu.VMEM((2, fields_dev, 2, 128), F32),
            pltpu.VMEM((2 * fields_dev * 8, 128), F32),
            pltpu.VMEM((strips, 8, 128), BF16),
            pltpu.VMEM((strips, 8, 128), BF16),
            pltpu.VMEM((strips, 8, 128), BF16),
            pltpu.VMEM((strips, 8, 128), BF16),
            pltpu.VMEM((strips, 8, 128), BF16),
            pltpu.VMEM((4, ADAM, 8, 128), F32),
            pltpu.VMEM((ADAM, strips, 8, 128), F32),
            pltpu.VMEM((ADAM, strips, 8, 128), F32),
            pltpu.VMEM((8, 128), BF16),
            pltpu.VMEM((ADAM, strips, 8, 128), BF16),
            pltpu.VMEM((8, in_weight.shape[1]), BF16),
            pltpu.VMEM((4, hidden_width // 4, points), BF16),
            dma((2,)),
            dma((2,)),
            dma((2,)),
            dma((1,)),
            dma((1,)),
            dma((1,)),
            dma((1,)),
            dma((3,)),
            dma((3,)),
            dma((ADAM,)),
            dma((ADAM,)),
            dma((1,)),
            dma((1,)),
            dma((ADAM, 3)),
            dma((ADAM, 3)),
            dma((1,)),
            dma((1,)),
        ],
        compiler_params=pltpu.CompilerParams(
            collective_id=0, has_side_effects=True, vmem_limit_bytes=48 * 1024 * 1024
        ),
        name="ensemble",
    )(
        initial,
        react_rates,
        jnp.transpose(snap_times),
        field_code,
        time_code,
        batch_ids,
        in_weight.reshape(strips, hidden_width // strips, in_weight.shape[1]),
        in_moment,
        in_second,
        out_weight.reshape(4, hidden_width // 4, points),
        out_moment,
        out_second,
    )
    fields, in_new, in_m, in_v, out_new, out_m, out_v = outs
    return (
        fields,
        in_new.reshape(in_weight.shape),
        in_m,
        in_v,
        out_new.reshape(out_weight.shape),
        out_m,
        out_v,
    )


def solution(mesh):
    in_specs = (
        P("group", "strip", None),
        P("group"),
        P(),
        P(),
        P(),
        P(None, "group"),
        P(),
        P("strip", None),
        P("strip", None),
        P(None, "strip"),
        P("group", "strip"),
        P("group", "strip"),
    )
    out_specs = (
        P("group", "strip", None),
        P(),
        P("strip", None),
        P("strip", None),
        P(None, "strip"),
        P("group", "strip"),
        P("group", "strip"),
    )
    return jax.shard_map(shards, mesh=mesh, in_specs=in_specs, out_specs=out_specs, check_vma=False)
```

time: 1840 us -> 89.7 us (0.05)
  the two profiles are of different devices: /device:TPU:1 before, /device:TPU:64 now
where the time goes in v1:
time: 89.7 us; the launch traced here: 89.2 us
  Pallas kernels  76 us (85%)
  local copies, waits for them, and re-layouts  12.5 us (14%)
    pallas_call x1, Pallas kernels, shards(): pl.pallas_call(kernel, out_shape=(jax.ShapeDtypeStruct(initial.shape, F32...  76 us
    unnamed x31, local copies, waits for them, and re-layouts  12.5 us

profile of v1, /device:TPU:64, one launch (start us, length us, event | category | flops | bytes accessed | tf_op | source)
XLA Modules:
  0.0 89.2 jit_solution(1065695812935836299)
XLA Ops:
  0.6 0.0 copy-start.9
  0.6 0.0 copy-start.8
  0.7 0.0 copy-start.10
  0.7 0.0 copy-start.11
  0.7 0.6 copy-done.9
  1.3 0.0 copy-done.8
  1.3 0.0 copy-done.10
  1.3 0.0 copy-done.11
  1.4 0.0 copy-start
  1.4 1.0 %copy-done = bf16[512,512]{1,0:T(8,128)(2,1)S(1)} copy-done((bf16[512,512]{1,0:T(8,128)(2,1)S(1)}, bf16[512,512]{1,0:T(8,128)(2,1)}, u32[]{:S(2)}) %copy-start) | copy-done | bytes 524312
  2.4 0.0 copy-start.1
  2.4 1.0 %copy-done.1 = bf16[512,512]{1,0:T(8,128)(2,1)S(1)} copy-done((bf16[512,512]{1,0:T(8,128)(2,1)S(1)}, bf16[512,512]{1,0:T(8,128)(2,1)}, u32[]{:S(2)}) %copy-start.1) | copy-done | bytes 524312
  3.4 0.0 copy-start.2
  3.4 0.9 %copy-done.2 = f32[128,512]{1,0:T(8,128)S(1)} copy-done((f32[128,512]{1,0:T(8,128)S(1)}, f32[128,512]{1,0:T(8,128)}, u32[]{:S(2)}) %copy-start.2) | copy-done | bytes 262168
  4.4 0.0 copy-start.3
  4.4 0.9 %copy-done.3 = f32[128,512]{1,0:T(8,128)S(1)} copy-done((f32[128,512]{1,0:T(8,128)S(1)}, f32[128,512]{1,0:T(8,128)}, u32[]{:S(2)}) %copy-start.3) | copy-done | bytes 262168
  5.3 0.0 copy-start.4
  5.3 0.8 copy-done.4
  6.2 0.0 copy-start.5
  6.2 0.8 copy-done.5
  6.9 0.0 copy-start.6
  6.9 0.7 copy-done.6
  7.7 0.0 copy-start.7
  7.7 0.7 copy-done.7
  8.4 76.0 %ensemble.1 = (f32[16,4,128]{2,1,0:T(4,128)S(1)}, bf16[64,8,512]{2,1,0:T(8,128)(2,1)S(1)}, f32[8,512]{1,0:T(8,128)S(1)}, f32[8,512]{1,0:T(8,128)S(1)}, bf16[4,12...) custom-call(f32[16,4,128]{2,1,0:T(4,128)S(1)} %copy-done.5, f32[16]{0:T(128)S(1)} %copy-done.11, ...), custom_call_target="tpu_custom_call" | custom-call | tf_op jit(solution)/shard_map/ensemble/pallas_call | solution.py:401
  84.4 0.6 copy.26
  85.0 0.8 copy.27
  85.8 0.6 copy.28
  86.4 0.6 copy.29
  87.0 0.8 copy.30
  87.8 0.7 copy.31
  88.5 0.7 copy.32
Async XLA Ops:
  0.6 0.7 copy-start.9
  0.6 0.7 copy-start.8
  0.7 0.7 copy-start.10
  0.7 0.7 copy-start.11
  1.4 1.0 %copy-start = (bf16[512,512]{1,0:T(8,128)(2,1)S(1)}, bf16[512,512]{1,0:T(8,128)(2,1)}, u32[]{:S(2)}) copy-start(bf16[512,512]{1,0:T(8,128)(2,1)} %param.18) | copy-start | bytes 1572868
  2.4 1.0 %copy-start.1 = (bf16[512,512]{1,0:T(8,128)(2,1)S(1)}, bf16[512,512]{1,0:T(8,128)(2,1)}, u32[]{:S(2)}) copy-start(bf16[512,512]{1,0:T(8,128)(2,1)} %param.21) | copy-start | bytes 1572868
  3.4 0.9 %copy-start.2 = (f32[128,512]{1,0:T(8,128)S(1)}, f32[128,512]{1,0:T(8,128)}, u32[]{:S(2)}) copy-start(f32[128,512]{1,0:T(8,128)} %out_moment.1) | copy-start | bytes 786436
  4.4 0.9 %copy-start.3 = (f32[128,512]{1,0:T(8,128)S(1)}, f32[128,512]{1,0:T(8,128)}, u32[]{:S(2)}) copy-start(f32[128,512]{1,0:T(8,128)} %out_second.1) | copy-start | bytes 786436
  5.3 0.8 copy-start.4
  6.2 0.8 copy-start.5
  6.9 0.7 copy-start.6
  7.7 0.7 copy-start.7

commit v2 on v1

--- a/solution.py
+++ b/solution.py
@@ -67,6 +67,25 @@
 
 
 def kernel(
+    initial_hbm,
+    rates_hbm,
+    times_hbm,
+    field_code_hbm,
+    time_code_hbm,
+    batch_ids_hbm,
+    in_weight_hbm,
+    in_moment_hbm,
+    in_second_hbm,
+    out_weight_hbm,
+    out_moment_hbm,
+    out_second_hbm,
+    fields_out,
+    in_weight_new,
+    in_moment_new,
+    in_second_new,
+    out_weight_new,
+    out_moment_new,
+    out_second_new,
     initial,
     rates,
     times,
@@ -79,13 +98,6 @@
     out_weight,
     out_moment,
     out_second,
-    fields_out,
-    in_weight_new,
-    in_moment_new,
-    in_second_new,
-    out_weight_new,
-    out_moment_new,
-    out_second_new,
     edges,
     halo,
     states,
@@ -118,6 +130,7 @@
     weight_recv,
     row_send,
     row_recv,
+    load_sem,
 ):
     strips = lax.axis_size("strip")
     me = lax.axis_index("strip")
@@ -143,6 +156,28 @@
         copy.start()
         return copy
 
+    loads = [
+        pltpu.make_async_copy(source, target, load_sem.at[i])
+        for i, (source, target) in enumerate(
+            (
+                (initial_hbm, initial),
+                (batch_ids_hbm, batch_ids),
+                (times_hbm, times),
+                (field_code_hbm, field_code),
+                (time_code_hbm, time_code),
+                (in_weight_hbm, in_weight),
+                (rates_hbm, rates),
+                (out_weight_hbm, out_weight),
+                (in_moment_hbm, in_moment),
+                (in_second_hbm, in_second),
+                (out_moment_hbm, out_moment),
+                (out_second_hbm, out_second),
+            )
+        )
+    ]
+    for load in loads:
+        load.start()
+
     barrier = pltpu.get_barrier_semaphore()
 
     def greet(strip, group):
@@ -160,6 +195,8 @@
     greet(me, mate)
     greet(me, far_mate)
 
+    for load in loads[:3]:
+        load.wait()
     edges[0] = initial[:, 0:2, :]
     edges[1] = initial[:, 2:4, :]
 
@@ -178,19 +215,8 @@
         hits = (batch_ids[turn : turn + 1, :] == field_row).astype(F32).astype(BF16)
         counts[0, turn] = dot(ones, hits, 1, 1) * time_fits
 
-    pl.semaphore_wait(barrier, 2 * others + 3)
-
-    up = lax.rem(me + others, strips)
-    down = lax.rem(me + 1, strips)
-    halo_copies = [
-        send(edges.at[0], halo.at[1], halo_send.at[0], halo_recv.at[1], up, g),
-        send(edges.at[1], halo.at[0], halo_send.at[1], halo_recv.at[0], down, g),
-    ]
-    count_copies = [
-        send(counts.at[0], counts.at[1 + i], count_send.at[i], count_recv.at[i], me, group)
-        for i, group in enumerate((far, mate, far_mate))
-    ]
-
+    for load in loads[3:6]:
+        load.wait()
     code_parts = []
     for part in range(4):
         for step in range(STEPS):
@@ -205,6 +231,22 @@
     pre_act = dot(in_weight[...].reshape(hidden_width, 512), code, 1, 1)
     hidden = gelu_value(pre_act).astype(BF16)
     hidden_all[0] = hidden.reshape(strips, 8, 128)
+
+    pl.semaphore_wait(barrier, 2 * others + 3)
+
+    up = lax.rem(me + others, strips)
+    down = lax.rem(me + 1, strips)
+    halo_copies = [
+        send(edges.at[0], halo.at[1], halo_send.at[0], halo_recv.at[1], up, g),
+        send(edges.at[1], halo.at[0], halo_send.at[1], halo_recv.at[0], down, g),
+    ]
+    count_copies = [
+        send(counts.at[0], counts.at[1 + i], count_send.at[i], count_recv.at[i], me, group)
+        for i, group in enumerate((far, mate, far_mate))
+    ]
+
+    for load in loads[6:]:
+        load.wait()
     old_weight = out_weight[...].reshape(hidden_width, 512)
     predict = dot(hidden, old_weight, 0, 0)
     own_pre = dot(in_weight[me], code, 1, 1)
@@ -377,6 +419,22 @@
     far_all.wait_send()
 
 
+def keep(sources, targets, sem):
+    copies = [
+        pltpu.make_async_copy(source, target, sem.at[i])
+        for i, (source, target) in enumerate(zip(sources, targets))
+    ]
+    for copy in copies:
+        copy.start()
+    for copy in copies:
+        copy.wait()
+
+
+def store(*refs):
+    count = len(refs) // 2
+    keep(refs[:count], refs[count : 2 * count], refs[-1])
+
+
 def shards(
     initial,
     react_rates,
@@ -396,22 +454,34 @@
     hidden_width = in_weight.shape[0]
     points = out_weight.shape[1]
     vmem = pl.BlockSpec(memory_space=pltpu.VMEM)
-    smem = pl.BlockSpec(memory_space=pltpu.SMEM)
+    hbm = pl.BlockSpec(memory_space=pltpu.HBM)
     dma = pltpu.SemaphoreType.DMA
     outs = pl.pallas_call(
         kernel,
         out_shape=(
-            jax.ShapeDtypeStruct(initial.shape, F32),
-            jax.ShapeDtypeStruct((strips, 8, in_weight.shape[1]), BF16),
-            jax.ShapeDtypeStruct(in_moment.shape, F32),
-            jax.ShapeDtypeStruct(in_second.shape, F32),
-            jax.ShapeDtypeStruct((4, hidden_width // 4, points), BF16),
-            jax.ShapeDtypeStruct(out_moment.shape, F32),
-            jax.ShapeDtypeStruct(out_second.shape, F32),
+            pltpu.VMEM(initial.shape, F32),
+            pltpu.VMEM((strips, 8, in_weight.shape[1]), BF16),
+            pltpu.VMEM(in_moment.shape, F32),
+            pltpu.VMEM(in_second.shape, F32),
+            pltpu.VMEM((4, hidden_width // 4, points), BF16),
+            pltpu.VMEM(out_moment.shape, F32),
+            pltpu.VMEM(out_second.shape, F32),
         ),
-        in_specs=[vmem, smem] + [vmem] * 10,
+        in_specs=[hbm] * 12,
         out_specs=(vmem,) * 7,
         scratch_shapes=[
+            pltpu.VMEM(initial.shape, F32),
+            pltpu.SMEM(react_rates.shape, F32),
+            pltpu.VMEM(snap_times.shape[::-1], jnp.int32),
+            pltpu.VMEM(field_code.shape, BF16),
+            pltpu.VMEM(time_code.shape, BF16),
+            pltpu.VMEM(batch_ids.shape, jnp.int32),
+            pltpu.VMEM((strips, 8, in_weight.shape[1]), BF16),
+            pltpu.VMEM(in_moment.shape, F32),
+            pltpu.VMEM(in_second.shape, F32),
+            pltpu.VMEM((4, hidden_width // 4, points), BF16),
+            pltpu.VMEM(out_moment.shape, F32),
+            pltpu.VMEM(out_second.shape, F32),
             pltpu.VMEM((2, fields_dev, 2, 128), F32),
             pltpu.VMEM((2, fields_dev, 2, 128), F32),
             pltpu.VMEM((2 * fields_dev * 8, 128), F32),
@@ -444,12 +514,16 @@
             dma((ADAM, 3)),
             dma((1,)),
             dma((1,)),
+            dma((12,)),
         ],
         compiler_params=pltpu.CompilerParams(
             collective_id=0, has_side_effects=True, vmem_limit_bytes=48 * 1024 * 1024
         ),
         name="ensemble",
     )(
+        *(
+            pltpu.with_memory_space_constraint(operand, pltpu.HBM)
+            for operand in (
         initial,
         react_rates,
         jnp.transpose(snap_times),
@@ -462,7 +536,17 @@
         out_weight.reshape(4, hidden_width // 4, points),
         out_moment,
         out_second,
-    )
+            )
+        )
+    )
+    outs = pl.pallas_call(
+        store,
+        out_shape=tuple(pltpu.HBM(out.shape, out.dtype) for out in outs),
+        in_specs=[vmem] * 7,
+        out_specs=(hbm,) * 7,
+        scratch_shapes=[dma((7,))],
+        name="store",
+    )(*(pltpu.with_memory_space_constraint(out, pltpu.VMEM) for out in outs))
     fields, in_new, in_m, in_v, out_new, out_m, out_v = outs
     return (
         fields,

time: 89.7 us -> 77.6 us (0.87)
  local copies, waits for them, and re-layouts: 12.5 us -> 0 us
  Pallas kernels: 76 us -> 76.9 us
    unnamed x31 -> x0, local copies, waits for them, and re-layouts: 12.5 us -> none
    pallas_call x1 -> x2, Pallas kernels: 76 us -> 76.9 us  [the longest x1 75.6 us: shards(): pl.pallas_call(kernel, out_shape=(pltpu.VMEM(initial.shape, F32), pltpu.V...]
where the time goes in v2:
time: 77.6 us; the launch traced here: 77.5 us
  Pallas kernels  76.9 us (99%)
    pallas_call x1, Pallas kernels, shards(): pl.pallas_call(kernel, out_shape=(pltpu.VMEM(initial.shape, F32), pltpu.V...  75.6 us

profile of v2, /device:TPU:64, one launch (start us, length us, event | category | flops | bytes accessed | tf_op | source)
XLA Modules:
  0.0 77.5 jit_solution(14206736359740667441)
XLA Ops:
  0.6 75.6 %ensemble.1 = (f32[16,4,128]{2,1,0:T(4,128)S(1)}, bf16[64,8,512]{2,1,0:T(8,128)(2,1)S(1)}, f32[8,512]{1,0:T(8,128)S(1)}, f32[8,512]{1,0:T(8,128)S(1)}, bf16[4,12...) custom-call(f32[16,4,128]{2,1,0:T(4,128)} %initial_hbm.1, f32[16]{0:T(128)} %rates_hbm.1, ...), custom_call_target="tpu_custom_call" | custom-call | tf_op jit(solution)/shard_map/ensemble/pallas_call | solution.py:459
  76.3 1.2 %store.1 = (f32[16,4,128]{2,1,0:T(4,128)}, bf16[64,8,512]{2,1,0:T(8,128)(2,1)}, f32[8,512]{1,0:T(8,128)}, f32[8,512]{1,0:T(8,128)}, bf16[4,128,512]{2,1,0:T(8,12...) custom-call(f32[16,4,128]{2,1,0:T(4,128)S(1)} %get-tuple-element.21.refs_0_, ...), custom_call_target="tpu_custom_call" | custom-call | tf_op jit(solution)/shard_map/store/pallas_call | solution.py:542

commit v3 on v2

--- a/solution.py
+++ b/solution.py
@@ -102,16 +102,14 @@
     halo,
     states,
     pieces,
-    from_own,
-    from_far,
-    half_pool,
-    core_pool,
+    arrived,
     counts,
     terms,
-    term_in,
+    plane_in,
+    line_out,
+    line_in,
     hidden_own,
     hidden_all,
-    rows_own,
     weight_mid,
     halo_send,
     halo_recv,
@@ -122,8 +120,10 @@
     pool_recv,
     count_send,
     count_recv,
-    term_send,
-    term_recv,
+    plane_send,
+    plane_recv,
+    line_send,
+    line_recv,
     hidden_send,
     hidden_recv,
     weight_send,
@@ -140,6 +140,7 @@
     far_mate = lax.rem(mate + 2, 4)
     fields = initial.shape[0]
     others = strips - 1
+    at_y, at_z, at_x = me // 16, lax.rem(me // 4, 4), lax.rem(me, 4)
 
     def other(k):
         return lax.rem(me + 1 + k, strips)
@@ -275,23 +276,33 @@
         states[8 * (fields + field) : 8 * (fields + field) + 8, :] = second
         fields_out[field] = second[2:6, :]
 
-    place_row = lax.broadcasted_iota(jnp.int32, (32, 128), 0)
-    place_lane = lax.broadcasted_iota(jnp.int32, (32, 128), 1)
-    place = (place_lane == place_row + 32 * g).astype(F32).astype(BF16)
+    def grid(shape):
+        return (lax.broadcasted_iota(jnp.int32, shape, i) for i in range(2))
+
+    def one_hot(hit):
+        return jnp.where(hit, 1.0, 0.0).astype(BF16)
+
+    kind_at, lane_at = grid((32, 128))
+    repeat = one_hot(kind_at == lax.rem(lane_at, 32))
+    point_at, lane_at = grid((128, 128))
+    own_lanes = lax.rem(point_at, 4) == lane_at // 32
+    four_at, point_at = grid((32, 128))
+    fold = one_hot(four_at == point_at // 4)
     for line in range(4):
         chosen = states[pl.ds(2 + line, 32, stride=8), :].astype(BF16)
-        piece = dot(chosen, place, 0, 0).astype(BF16)
-        pieces[16 * line : 16 * line + 16] = piece.reshape(16, 8, 128)
+        spread_out = jnp.where(own_lanes, dot(chosen, repeat, 0, 0), 0.0).astype(BF16)
+        piece = dot(fold, spread_out, 1, 0)
+        pieces[16 * line : 16 * line + 16] = piece.reshape(16, 2, 128).astype(BF16)
 
     def send_piece(k, carry):
         t = other(k)
-        send(pieces.at[t], from_own.at[me], piece_send.at[0], own_recv.at[0], t, g)
-        send(pieces.at[t], from_far.at[me], piece_send.at[1], far_recv.at[0], t, far)
+        send(pieces.at[t], arrived.at[0, me], piece_send.at[0], own_recv.at[0], t, g)
+        send(pieces.at[t], arrived.at[1, me], piece_send.at[1], far_recv.at[0], t, far)
         return carry
 
     lax.fori_loop(0, others, send_piece, 0)
-    send(pieces.at[me], from_far.at[me], piece_send.at[1], far_recv.at[0], me, far)
-    from_own[me] = pieces[me]
+    send(pieces.at[me], arrived.at[1, me], piece_send.at[1], far_recv.at[0], me, far)
+    arrived[0, me] = pieces[me]
 
     def whole(source, target, send_sem, recv_sem):
         return pltpu.make_async_remote_copy(
@@ -304,17 +315,30 @@
         )
 
     most = pl.ds(0, others)
-    own_all = whole(pieces.at[most], from_own.at[most], piece_send.at[0], own_recv.at[0])
-    far_all = whole(pieces, from_far, piece_send.at[1], far_recv.at[0])
+    own_all = whole(pieces.at[most], arrived.at[0, most], piece_send.at[0], own_recv.at[0])
+    far_all = whole(pieces, arrived.at[1], piece_send.at[1], far_recv.at[0])
     own_all.wait_recv()
     far_all.wait_recv()
-    half_pool[...] = from_own[...] + from_far[...]
-    pool_copy = send(half_pool, core_pool, pool_send.at[0], pool_recv.at[0], me, mate)
+    pool_copy = send(
+        arrived.at[pl.ds(0, 2)], arrived.at[pl.ds(2, 2)], pool_send.at[0], pool_recv.at[0], me, mate
+    )
     for copy in count_copies:
         copy.wait()
     count = jnp.sum(counts[...], axis=0)
+    point_at, row_at = grid((8 * strips, 2 * strips))
+    unfold = one_hot(point_at // 4 == row_at)
+    point_at, lane_at = grid((8 * strips, 128))
+    own_lanes = lax.rem(point_at, 4) == lane_at // 32
+    lane_at, kind_at = grid((128, 128))
+
+    def pool_of(part, group):
+        rows = arrived[part].astype(F32).reshape(2 * strips, 128).astype(BF16)
+        points = jnp.where(own_lanes, dot(unfold, rows, 1, 0), 0.0).astype(BF16)
+        return dot(one_hot(kind_at == 32 * group + lax.rem(lane_at, 32)), points, 0, 1)
+
+    pool = pool_of(0, g) + pool_of(1, far)
     pool_copy.wait()
-    pool = (half_pool[...] + core_pool[...]).reshape(8 * strips, 128).astype(F32).T
+    pool = pool + pool_of(2, mate) + pool_of(3, far_mate)
 
     moment, second_moment = out_moment[...], out_second[...]
     row_weight, row_moment, row_second = in_weight[me], in_moment[...], in_second[...]
@@ -323,24 +347,7 @@
         step_count = PRIOR + turn + 1
         number = count[turn, 0:1, :]
         delta = ((predict - pool) * (1.0 / 512.0)).astype(BF16)
-        terms[turn] = dot(current[...].reshape(hidden_width, 512), delta, 1, 1).reshape(
-            strips, 8, 128
-        )
-
-        def send_terms(k, carry):
-            t = other(k)
-            send(
-                terms.at[turn, t],
-                term_in.at[turn, me],
-                term_send.at[turn],
-                term_recv.at[turn],
-                t,
-                g,
-            )
-            return carry
-
-        lax.fori_loop(0, others, send_terms, 0)
-        term_in[turn, me] = terms[turn, me]
+        weights = current[...].reshape(hidden_width, 512)
 
         own_hidden = hidden_all[turn, pl.ds(g * (strips // 4), strips // 4)].reshape(
             hidden_width // 4, 128
@@ -351,23 +358,62 @@
         )
         following = weight_mid if turn + 1 < ADAM else out_weight_new
         following[g] = new_rows
-        weight_copies = [
-            send(
-                following.at[g],
-                following.at[g],
+
+        def weight_copy(part, i, group):
+            return send(
+                following.at[part],
+                following.at[part],
                 weight_send.at[turn, i],
                 weight_recv.at[turn, i],
                 me,
                 group,
             )
-            for i, group in enumerate((far, mate))
-        ]
-
-        term_all = whole(
-            terms.at[turn, most], term_in.at[turn, most], term_send.at[turn], term_recv.at[turn]
-        )
-        term_all.wait_recv()
-        hidden_grad = jnp.sum(term_in[turn], axis=0)
+
+        def start_weight():
+            return [weight_copy(g, 0, far), weight_copy(g, 1, mate)]
+
+        weight_copies = start_weight()
+        terms[turn] = dot(weights, delta, 1, 1).reshape(4, 4, 4, 8, 128)
+
+        def send_terms(k, carry):
+            ty = lax.rem(at_y + (k + 1) // 4, 4)
+            tx = lax.rem(at_x + lax.rem(k + 1, 4), 4)
+            send(
+                terms.at[turn, ty, :, tx],
+                plane_in.at[turn, 4 * at_y + at_x],
+                plane_send.at[turn],
+                plane_recv.at[turn],
+                16 * ty + 4 * at_z + tx,
+                g,
+            )
+            return carry
+
+        lax.fori_loop(0, 15, send_terms, 0)
+        plane_in[turn, 4 * at_y + at_x] = terms[turn, at_y, :, at_x]
+        plane = plane_in.at[turn, pl.ds(0, 15)]
+        plane_all = whole(plane, plane, plane_send.at[turn], plane_recv.at[turn])
+        plane_all.wait_recv()
+        line_out[turn] = jnp.sum(plane_in[turn], axis=0)
+
+        def send_line(k, carry):
+            tz = lax.rem(at_z + k + 1, 4)
+            send(
+                line_out.at[turn, tz],
+                line_in.at[turn, at_z],
+                line_send.at[turn],
+                line_recv.at[turn],
+                16 * at_y + 4 * tz + at_x,
+                g,
+            )
+            return carry
+
+        lax.fori_loop(0, 3, send_line, 0)
+        line_in[turn, at_z] = line_out[turn, at_z]
+        line = line_in.at[turn, pl.ds(0, 3)]
+        line_all = whole(line, line, line_send.at[turn], line_recv.at[turn])
+        line_all.wait_recv()
+
+        hidden_grad = jnp.sum(line_in[turn], axis=0)
         pre_grad = (hidden_grad * gelu_slope(own_pre)).astype(BF16)
         in_grad = sum(dot(part, code, 1, 0) for part in three_parts(pre_grad.astype(F32) * number))
         row_weight, row_moment, row_second = adam_update(
@@ -376,16 +422,24 @@
         if turn + 1 < ADAM:
             own_pre = dot(row_weight, code, 1, 1)
             hidden_own[...] = gelu_value(own_pre).astype(BF16)
-            source, gathered, send_sem, recv_sem = hidden_own, hidden_all.at[1], hidden_send, hidden_recv
             hidden_all[1, me] = hidden_own[...]
+            source, target, several = hidden_own, hidden_all.at[1, me], hidden_all.at[1, most]
+            send_sem, recv_sem = hidden_send, hidden_recv
         else:
-            rows_own[...] = row_weight
-            source, gathered, send_sem, recv_sem = rows_own, in_weight_new, row_send, row_recv
-            in_weight_new[me] = row_weight
+            half = pl.ds(pl.multiple_of(256 * lax.rem(g, 2), 256), 256)
+            in_weight_new[me, :, half] = jnp.where(
+                lax.rem(g, 2) == 0,
+                row_weight[:, :256].astype(F32),
+                row_weight[:, 256:].astype(F32),
+            ).astype(BF16)
+            source = target = in_weight_new.at[me, :, half]
+            several = in_weight_new.at[most, :, half]
+            send_sem, recv_sem = row_send, row_recv
+
 
         def send_rows(k, carry):
             t = other(k)
-            send(source, gathered.at[me], send_sem.at[0], recv_sem.at[0], t, g)
+            send(source, target, send_sem.at[0], recv_sem.at[0], t, g)
             return carry
 
         lax.fori_loop(0, others, send_rows, 0)
@@ -394,19 +448,17 @@
             in_second_new[...] = row_second
             out_moment_new[...] = moment
             out_second_new[...] = second_moment
-        for copy in weight_copies:
+        weight_copies[0].wait()
+        weight_copies.append(weight_copy(far, 2, mate))
+        rows_all = whole(several, several, send_sem.at[0], recv_sem.at[0])
+        rows_all.wait()
+        if turn + 1 == ADAM:
+            columns = in_weight_new.at[:, :, half]
+            send(columns, columns, row_send.at[1], row_recv.at[1], me, mate).wait()
+        for copy in weight_copies[1:]:
             copy.wait()
-        send(
-            following.at[far],
-            following.at[far],
-            weight_send.at[turn, 2],
-            weight_recv.at[turn, 2],
-            me,
-            mate,
-        ).wait()
-        rows_all = whole(gathered.at[most], gathered.at[most], send_sem.at[0], recv_sem.at[0])
-        rows_all.wait()
-        term_all.wait_send()
+        plane_all.wait_send()
+        line_all.wait_send()
         if turn + 1 < ADAM:
             current = following
             predict = dot(
@@ -485,17 +537,15 @@
             pltpu.VMEM((2, fields_dev, 2, 128), F32),
             pltpu.VMEM((2, fields_dev, 2, 128), F32),
             pltpu.VMEM((2 * fields_dev * 8, 128), F32),
-            pltpu.VMEM((strips, 8, 128), BF16),
-            pltpu.VMEM((strips, 8, 128), BF16),
-            pltpu.VMEM((strips, 8, 128), BF16),
-            pltpu.VMEM((strips, 8, 128), BF16),
-            pltpu.VMEM((strips, 8, 128), BF16),
+            pltpu.VMEM((strips, 2, 128), BF16),
+            pltpu.VMEM((4, strips, 2, 128), BF16),
             pltpu.VMEM((4, ADAM, 8, 128), F32),
-            pltpu.VMEM((ADAM, strips, 8, 128), F32),
-            pltpu.VMEM((ADAM, strips, 8, 128), F32),
+            pltpu.VMEM((ADAM, 4, 4, 4, 8, 128), F32),
+            pltpu.VMEM((ADAM, 16, 4, 8, 128), F32),
+            pltpu.VMEM((ADAM, 4, 8, 128), F32),
+            pltpu.VMEM((ADAM, 4, 8, 128), F32),
             pltpu.VMEM((8, 128), BF16),
             pltpu.VMEM((ADAM, strips, 8, 128), BF16),
-            pltpu.VMEM((8, in_weight.shape[1]), BF16),
             pltpu.VMEM((4, hidden_width // 4, points), BF16),
             dma((2,)),
             dma((2,)),
@@ -508,12 +558,14 @@
             dma((3,)),
             dma((ADAM,)),
             dma((ADAM,)),
+            dma((ADAM,)),
+            dma((ADAM,)),
             dma((1,)),
             dma((1,)),
             dma((ADAM, 3)),
             dma((ADAM, 3)),
-            dma((1,)),
-            dma((1,)),
+            dma((2,)),
+            dma((2,)),
             dma((12,)),
         ],
         compiler_params=pltpu.CompilerParams(

time: 77.6 us -> 66.8 us (0.86)
  the two profiles are of different devices: /device:TPU:64 before, /device:TPU:1 now
where the time goes in v3:
time: 66.8 us; the launch traced here: 66.7 us
  Pallas kernels  66.1 us (99%)
    pallas_call x1, Pallas kernels, shards(): pl.pallas_call(kernel, out_shape=(pltpu.VMEM(initial.shape, F32), pltpu.V...  64.9 us

profile of v3, /device:TPU:1, one launch (start us, length us, event | category | flops | bytes accessed | tf_op | source)
XLA Modules:
  0.0 66.7 jit_solution(7200936691552182026)
XLA Ops:
  0.6 64.9 %ensemble.1 = (f32[16,4,128]{2,1,0:T(4,128)S(1)}, bf16[64,8,512]{2,1,0:T(8,128)(2,1)S(1)}, f32[8,512]{1,0:T(8,128)S(1)}, f32[8,512]{1,0:T(8,128)S(1)}, bf16[4,12...) custom-call(f32[16,4,128]{2,1,0:T(4,128)} %initial_hbm.1, f32[16]{0:T(128)} %rates_hbm.1, ...), custom_call_target="tpu_custom_call" | custom-call | tf_op jit(solution)/shard_map/ensemble/pallas_call | solution.py:511
  65.5 1.2 %store.1 = (f32[16,4,128]{2,1,0:T(4,128)}, bf16[64,8,512]{2,1,0:T(8,128)(2,1)}, f32[8,512]{1,0:T(8,128)}, f32[8,512]{1,0:T(8,128)}, bf16[4,128,512]{2,1,0:T(8,12...) custom-call(f32[16,4,128]{2,1,0:T(4,128)S(1)} %get-tuple-element.21.refs_0_, ...), custom_call_target="tpu_custom_call" | custom-call | tf_op jit(solution)/shard_map/store/pallas_call | solution.py:594

commit v4 on v3

--- a/solution.py
+++ b/solution.py
@@ -131,6 +131,9 @@
     row_send,
     row_recv,
     load_sem,
+    swap_send,
+    swap_recv,
+    plane_in_kernel,
 ):
     strips = lax.axis_size("strip")
     me = lax.axis_index("strip")
@@ -141,6 +144,16 @@
     fields = initial.shape[0]
     others = strips - 1
     at_y, at_z, at_x = me // 16, lax.rem(me // 4, 4), lax.rem(me, 4)
+
+    def each(count, body):
+        width = 7 if count % 7 == 0 else 1
+
+        def steps(k, carry):
+            for i in range(width):
+                body(width * k + i)
+            return carry
+
+        lax.fori_loop(0, count // width, steps, 0)
 
     def other(k):
         return lax.rem(me + 1 + k, strips)
@@ -186,15 +199,20 @@
             barrier, inc=1, device_id={"strip": strip, "group": group}, device_id_type=MESH
         )
 
-    def greet_strip(k, carry):
-        greet(other(k), g)
-        greet(other(k), far)
-        return carry
-
-    lax.fori_loop(0, others, greet_strip, 0)
-    greet(me, far)
-    greet(me, mate)
-    greet(me, far_mate)
+    plane_peers = []
+    line_peers = []
+    for i in range(1, 16):
+        ty, tx = lax.rem(at_y + i // 4, 4), lax.rem(at_x + i % 4, 4)
+        plane_peers.append((16 * ty + 4 * at_z + tx, g))
+    for i in range(1, 4):
+        strip = 16 * at_y + 4 * lax.rem(at_z + i, 4) + at_x
+        line_peers += [(strip, far), (strip, g)]
+    line_peers.append((me, far))
+    up = lax.rem(me + others, strips)
+    down = lax.rem(me + 1, strips)
+    for strip, group in [(up, g), (down, g)] + line_peers + plane_peers + [(me, mate), (me, far_mate)]:
+        greet(strip, group)
+    greeted = 26
 
     for load in loads[:3]:
         load.wait()
@@ -233,10 +251,8 @@
     hidden = gelu_value(pre_act).astype(BF16)
     hidden_all[0] = hidden.reshape(strips, 8, 128)
 
-    pl.semaphore_wait(barrier, 2 * others + 3)
-
-    up = lax.rem(me + others, strips)
-    down = lax.rem(me + 1, strips)
+    pl.semaphore_wait(barrier, greeted)
+
     halo_copies = [
         send(edges.at[0], halo.at[1], halo_send.at[0], halo_recv.at[1], up, g),
         send(edges.at[1], halo.at[0], halo_send.at[1], halo_recv.at[0], down, g),
@@ -248,6 +264,13 @@
 
     for load in loads[6:]:
         load.wait()
+    for strip, group in line_peers:
+        pl.semaphore_signal(
+            plane_in_kernel,
+            inc=1,
+            device_id={"strip": strip, "group": group},
+            device_id_type=MESH,
+        )
     old_weight = out_weight[...].reshape(hidden_width, 512)
     predict = dot(hidden, old_weight, 0, 0)
     own_pre = dot(in_weight[me], code, 1, 1)
@@ -294,13 +317,13 @@
         piece = dot(fold, spread_out, 1, 0)
         pieces[16 * line : 16 * line + 16] = piece.reshape(16, 2, 128).astype(BF16)
 
-    def send_piece(k, carry):
+    pl.semaphore_wait(plane_in_kernel, 7)
+    def send_piece(k):
         t = other(k)
         send(pieces.at[t], arrived.at[0, me], piece_send.at[0], own_recv.at[0], t, g)
         send(pieces.at[t], arrived.at[1, me], piece_send.at[1], far_recv.at[0], t, far)
-        return carry
-
-    lax.fori_loop(0, others, send_piece, 0)
+
+    each(others, send_piece)
     send(pieces.at[me], arrived.at[1, me], piece_send.at[1], far_recv.at[0], me, far)
     arrived[0, me] = pieces[me]
 
@@ -328,17 +351,24 @@
     point_at, row_at = grid((8 * strips, 2 * strips))
     unfold = one_hot(point_at // 4 == row_at)
     point_at, lane_at = grid((8 * strips, 128))
-    own_lanes = lax.rem(point_at, 4) == lane_at // 32
-    lane_at, kind_at = grid((128, 128))
-
-    def pool_of(part, group):
-        rows = arrived[part].astype(F32).reshape(2 * strips, 128).astype(BF16)
-        points = jnp.where(own_lanes, dot(unfold, rows, 1, 0), 0.0).astype(BF16)
-        return dot(one_hot(kind_at == 32 * group + lax.rem(lane_at, 32)), points, 0, 1)
-
-    pool = pool_of(0, g) + pool_of(1, far)
+    lane_at2 = lax.broadcasted_iota(jnp.int32, (8 * strips, 256), 1)
+    own_lanes = lax.rem(lax.broadcasted_iota(jnp.int32, (8 * strips, 256), 0), 4) == (
+        lax.rem(lane_at2, 128) // 32
+    )
+    lane_at, kind_at = grid((256, 128))
+
+    def pool_of(part, group, other_group):
+        rows = [
+            arrived[part + i].astype(F32).reshape(2 * strips, 128).astype(BF16) for i in range(2)
+        ]
+        points = dot(unfold, jnp.concatenate(rows, axis=1), 1, 0)
+        points = jnp.where(own_lanes, points, 0.0).astype(BF16)
+        start = jnp.where(lane_at < 128, 32 * group, 32 * other_group)
+        return dot(one_hot(kind_at == start + lax.rem(lane_at, 32)), points, 0, 1)
+
+    pool = pool_of(0, g, far)
     pool_copy.wait()
-    pool = pool + pool_of(2, mate) + pool_of(3, far_mate)
+    pool = pool + pool_of(2, mate, far_mate)
 
     moment, second_moment = out_moment[...], out_second[...]
     row_weight, row_moment, row_second = in_weight[me], in_moment[...], in_second[...]
@@ -375,7 +405,7 @@
         weight_copies = start_weight()
         terms[turn] = dot(weights, delta, 1, 1).reshape(4, 4, 4, 8, 128)
 
-        def send_terms(k, carry):
+        def send_terms(k):
             ty = lax.rem(at_y + (k + 1) // 4, 4)
             tx = lax.rem(at_x + lax.rem(k + 1, 4), 4)
             send(
@@ -386,16 +416,15 @@
                 16 * ty + 4 * at_z + tx,
                 g,
             )
-            return carry
-
-        lax.fori_loop(0, 15, send_terms, 0)
+
+        each(15, send_terms)
         plane_in[turn, 4 * at_y + at_x] = terms[turn, at_y, :, at_x]
         plane = plane_in.at[turn, pl.ds(0, 15)]
         plane_all = whole(plane, plane, plane_send.at[turn], plane_recv.at[turn])
         plane_all.wait_recv()
         line_out[turn] = jnp.sum(plane_in[turn], axis=0)
 
-        def send_line(k, carry):
+        def send_line(k):
             tz = lax.rem(at_z + k + 1, 4)
             send(
                 line_out.at[turn, tz],
@@ -405,9 +434,8 @@
                 16 * at_y + 4 * tz + at_x,
                 g,
             )
-            return carry
-
-        lax.fori_loop(0, 3, send_line, 0)
+
+        each(3, send_line)
         line_in[turn, at_z] = line_out[turn, at_z]
         line = line_in.at[turn, pl.ds(0, 3)]
         line_all = whole(line, line, line_send.at[turn], line_recv.at[turn])
@@ -437,12 +465,11 @@
             send_sem, recv_sem = row_send, row_recv
 
 
-        def send_rows(k, carry):
+        def send_rows(k):
             t = other(k)
-            send(source, target, send_sem.at[0], recv_sem.at[0], t, g)
-            return carry
-
-        lax.fori_loop(0, others, send_rows, 0)
+            send(source, target, send_sem.at[0], recv_sem.at[at_y if turn + 1 == ADAM else 0], t, g)
+
+        each(others, send_rows)
         if turn + 1 == ADAM:
             in_moment_new[...] = row_moment
             in_second_new[...] = row_second
@@ -450,11 +477,19 @@
             out_second_new[...] = second_moment
         weight_copies[0].wait()
         weight_copies.append(weight_copy(far, 2, mate))
-        rows_all = whole(several, several, send_sem.at[0], recv_sem.at[0])
-        rows_all.wait()
         if turn + 1 == ADAM:
-            columns = in_weight_new.at[:, :, half]
-            send(columns, columns, row_send.at[1], row_recv.at[1], me, mate).wait()
+            swaps = []
+            for i, step in enumerate((0, 1, 3, 2)):
+                ty = lax.rem(at_y + step, 4)
+                some = in_weight_new.at[pl.ds(16 * ty, 15 if step == 0 else 16), :, half]
+                whole(some, some, send_sem.at[0], recv_sem.at[ty]).wait_recv()
+                some = in_weight_new.at[pl.ds(16 * ty, 16), :, half]
+                swaps.append(send(some, some, swap_send.at[i], swap_recv.at[i], me, mate))
+            for swap in swaps:
+                swap.wait()
+            whole(several, several, send_sem.at[0], recv_sem.at[0]).wait_send()
+        else:
+            whole(several, several, send_sem.at[0], recv_sem.at[0]).wait()
         for copy in weight_copies[1:]:
             copy.wait()
         plane_all.wait_send()
@@ -564,9 +599,12 @@
             dma((1,)),
             dma((ADAM, 3)),
             dma((ADAM, 3)),
-            dma((2,)),
-            dma((2,)),
+            dma((1,)),
+            dma((4,)),
             dma((12,)),
+            dma((4,)),
+            dma((4,)),
+            pltpu.SemaphoreType.REGULAR,
         ],
         compiler_params=pltpu.CompilerParams(
             collective_id=0, has_side_effects=True, vmem_limit_bytes=48 * 1024 * 1024

time: 66.8 us -> 64.9 us (0.972)
  Pallas kernels: 66.1 us -> 64.1 us
    pallas_call x1, Pallas kernels: 64.9 us -> 62.9 us  [shards(): pl.pallas_call(kernel, out_shape=(pltpu.VMEM(initial.shape, F32), pltpu.V...]
where the time goes in v4:
time: 64.9 us; the launch traced here: 64.8 us
  Pallas kernels  64.1 us (99%)
  between operations  0.65 us (1%)
    pallas_call x1, Pallas kernels, shards(): pl.pallas_call(kernel, out_shape=(pltpu.VMEM(initial.shape, F32), pltpu.V...  62.9 us

profile of v4, /device:TPU:1, one launch (start us, length us, event | category | flops | bytes accessed | tf_op | source)
XLA Modules:
  0.0 64.8 jit_solution(4935968406351337754)
XLA Ops:
  0.6 62.9 %ensemble.1 = (f32[16,4,128]{2,1,0:T(4,128)S(1)}, bf16[64,8,512]{2,1,0:T(8,128)(2,1)S(1)}, f32[8,512]{1,0:T(8,128)S(1)}, f32[8,512]{1,0:T(8,128)S(1)}, bf16[4,12...) custom-call(f32[16,4,128]{2,1,0:T(4,128)} %initial_hbm.1, f32[16]{0:T(128)} %rates_hbm.1, ...), custom_call_target="tpu_custom_call" | custom-call | tf_op jit(solution)/shard_map/ensemble/pallas_call | solution.py:546
  63.6 1.2 %store.1 = (f32[16,4,128]{2,1,0:T(4,128)}, bf16[64,8,512]{2,1,0:T(8,128)(2,1)}, f32[8,512]{1,0:T(8,128)}, f32[8,512]{1,0:T(8,128)}, bf16[4,128,512]{2,1,0:T(8,12...) custom-call(f32[16,4,128]{2,1,0:T(4,128)S(1)} %get-tuple-element.21.refs_0_, ...), custom_call_target="tpu_custom_call" | custom-call | tf_op jit(solution)/shard_map/store/pallas_call | solution.py:632

commit v5 on v4

--- a/solution.py
+++ b/solution.py
@@ -143,6 +143,7 @@
     far_mate = lax.rem(mate + 2, 4)
     fields = initial.shape[0]
     others = strips - 1
+    core = lax.rem(g, 2)
     at_y, at_z, at_x = me // 16, lax.rem(me // 4, 4), lax.rem(me, 4)
 
     def each(count, body):
@@ -379,30 +380,6 @@
         delta = ((predict - pool) * (1.0 / 512.0)).astype(BF16)
         weights = current[...].reshape(hidden_width, 512)
 
-        own_hidden = hidden_all[turn, pl.ds(g * (strips // 4), strips // 4)].reshape(
-            hidden_width // 4, 128
-        )
-        grad = sum(dot(part, delta, 1, 0) for part in three_parts(own_hidden.astype(F32) * number))
-        new_rows, moment, second_moment = adam_update(
-            current[g], moment, second_moment, grad, step_count
-        )
-        following = weight_mid if turn + 1 < ADAM else out_weight_new
-        following[g] = new_rows
-
-        def weight_copy(part, i, group):
-            return send(
-                following.at[part],
-                following.at[part],
-                weight_send.at[turn, i],
-                weight_recv.at[turn, i],
-                me,
-                group,
-            )
-
-        def start_weight():
-            return [weight_copy(g, 0, far), weight_copy(g, 1, mate)]
-
-        weight_copies = start_weight()
         terms[turn] = dot(weights, delta, 1, 1).reshape(4, 4, 4, 8, 128)
 
         def send_terms(k):
@@ -419,6 +396,32 @@
 
         each(15, send_terms)
         plane_in[turn, 4 * at_y + at_x] = terms[turn, at_y, :, at_x]
+
+        own_hidden = hidden_all[turn, pl.ds(g * (strips // 4), strips // 4)].reshape(
+            hidden_width // 4, 128
+        )
+        grad = sum(dot(part, delta, 1, 0) for part in three_parts(own_hidden.astype(F32) * number))
+        new_rows, moment, second_moment = adam_update(
+            current[g], moment, second_moment, grad, step_count
+        )
+        following = weight_mid if turn + 1 < ADAM else out_weight_new
+        following[g] = new_rows
+
+        def weight_copy(part, i, group):
+            return send(
+                following.at[part],
+                following.at[part],
+                weight_send.at[turn, i],
+                weight_recv.at[turn, i],
+                me,
+                group,
+            )
+
+        def start_weight():
+            return [weight_copy(g, 0, far), weight_copy(g, 1, mate)]
+
+        weight_copies = start_weight()
+        slope = gelu_slope(own_pre)
         plane = plane_in.at[turn, pl.ds(0, 15)]
         plane_all = whole(plane, plane, plane_send.at[turn], plane_recv.at[turn])
         plane_all.wait_recv()
@@ -442,8 +445,10 @@
         line_all.wait_recv()
 
         hidden_grad = jnp.sum(line_in[turn], axis=0)
-        pre_grad = (hidden_grad * gelu_slope(own_pre)).astype(BF16)
-        in_grad = sum(dot(part, code, 1, 0) for part in three_parts(pre_grad.astype(F32) * number))
+        pre_grad = (hidden_grad * slope).astype(BF16)
+        parts = [part.astype(F32) for part in three_parts(pre_grad.astype(F32) * number)]
+        in_grads = dot(jnp.concatenate(parts, axis=0).astype(BF16), code, 1, 0)
+        in_grad = in_grads[0:8] + in_grads[8:16] + in_grads[16:24]
         row_weight, row_moment, row_second = adam_update(
             row_weight, row_moment, row_second, in_grad, step_count
         )
@@ -454,20 +459,17 @@
             source, target, several = hidden_own, hidden_all.at[1, me], hidden_all.at[1, most]
             send_sem, recv_sem = hidden_send, hidden_recv
         else:
-            half = pl.ds(pl.multiple_of(256 * lax.rem(g, 2), 256), 256)
-            in_weight_new[me, :, half] = jnp.where(
-                lax.rem(g, 2) == 0,
-                row_weight[:, :256].astype(F32),
-                row_weight[:, 256:].astype(F32),
+            in_weight_new[core, me] = jnp.where(
+                core == 0, row_weight[:, :256].astype(F32), row_weight[:, 256:].astype(F32)
             ).astype(BF16)
-            source = target = in_weight_new.at[me, :, half]
-            several = in_weight_new.at[most, :, half]
+            source = target = in_weight_new.at[core, me]
+            several = in_weight_new.at[core, most]
             send_sem, recv_sem = row_send, row_recv
 
 
         def send_rows(k):
             t = other(k)
-            send(source, target, send_sem.at[0], recv_sem.at[at_y if turn + 1 == ADAM else 0], t, g)
+            send(source, target, send_sem.at[0], recv_sem.at[0], t, g)
 
         each(others, send_rows)
         if turn + 1 == ADAM:
@@ -477,19 +479,10 @@
             out_second_new[...] = second_moment
         weight_copies[0].wait()
         weight_copies.append(weight_copy(far, 2, mate))
+        whole(several, several, send_sem.at[0], recv_sem.at[0]).wait()
         if turn + 1 == ADAM:
-            swaps = []
-            for i, step in enumerate((0, 1, 3, 2)):
-                ty = lax.rem(at_y + step, 4)
-                some = in_weight_new.at[pl.ds(16 * ty, 15 if step == 0 else 16), :, half]
-                whole(some, some, send_sem.at[0], recv_sem.at[ty]).wait_recv()
-                some = in_weight_new.at[pl.ds(16 * ty, 16), :, half]
-                swaps.append(send(some, some, swap_send.at[i], swap_recv.at[i], me, mate))
-            for swap in swaps:
-                swap.wait()
-            whole(several, several, send_sem.at[0], recv_sem.at[0]).wait_send()
-        else:
-            whole(several, several, send_sem.at[0], recv_sem.at[0]).wait()
+            columns = in_weight_new.at[core]
+            send(columns, columns, swap_send.at[0], swap_recv.at[0], me, mate).wait()
         for copy in weight_copies[1:]:
             copy.wait()
         plane_all.wait_send()
@@ -506,20 +499,18 @@
     far_all.wait_send()
 
 
-def keep(sources, targets, sem):
+def store(*refs):
+    sources, targets, sem = refs[:7], refs[7:14], refs[14]
+    width = sources[1].shape[-1]
+    pairs = [(sources[1].at[i], targets[1].at[:, :, pl.ds(width * i, width)]) for i in range(2)]
+    pairs += [(sources[i], targets[i]) for i in (4, 5, 6, 0, 2, 3)]
     copies = [
-        pltpu.make_async_copy(source, target, sem.at[i])
-        for i, (source, target) in enumerate(zip(sources, targets))
+        pltpu.make_async_copy(source, target, sem.at[i]) for i, (source, target) in enumerate(pairs)
     ]
     for copy in copies:
         copy.start()
     for copy in copies:
         copy.wait()
-
-
-def store(*refs):
-    count = len(refs) // 2
-    keep(refs[:count], refs[count : 2 * count], refs[-1])
 
 
 def shards(
@@ -547,7 +538,7 @@
         kernel,
         out_shape=(
             pltpu.VMEM(initial.shape, F32),
-            pltpu.VMEM((strips, 8, in_weight.shape[1]), BF16),
+            pltpu.VMEM((2, strips, 8, in_weight.shape[1] // 2), BF16),
             pltpu.VMEM(in_moment.shape, F32),
             pltpu.VMEM(in_second.shape, F32),
             pltpu.VMEM((4, hidden_width // 4, points), BF16),
@@ -600,10 +591,10 @@
             dma((ADAM, 3)),
             dma((ADAM, 3)),
             dma((1,)),
-            dma((4,)),
+            dma((1,)),
             dma((12,)),
-            dma((4,)),
-            dma((4,)),
+            dma((1,)),
+            dma((1,)),
             pltpu.SemaphoreType.REGULAR,
         ],
         compiler_params=pltpu.CompilerParams(
@@ -631,10 +622,13 @@
     )
     outs = pl.pallas_call(
         store,
-        out_shape=tuple(pltpu.HBM(out.shape, out.dtype) for out in outs),
+        out_shape=tuple(
+            pltpu.HBM((strips, 8, in_weight.shape[1]) if i == 1 else out.shape, out.dtype)
+            for i, out in enumerate(outs)
+        ),
         in_specs=[vmem] * 7,
         out_specs=(hbm,) * 7,
-        scratch_shapes=[dma((7,))],
+        scratch_shapes=[dma((8,))],
         name="store",
     )(*(pltpu.with_memory_space_constraint(out, pltpu.VMEM) for out in outs))
     fields, in_new, in_m, in_v, out_new, out_m, out_v = outs

time: 64.9 us -> 64.8 us (level)
  no operation moved by 1% of the time
where the time goes in v5:
time: 64.8 us; the launch traced here: 64.7 us
  Pallas kernels  64 us (99%)
  between operations  0.65 us (1%)
    pallas_call x1, Pallas kernels, shards(): pl.pallas_call(kernel, out_shape=(pltpu.VMEM(initial.shape, F32), pltpu.V...  62.8 us

profile of v5, /device:TPU:1, one launch (start us, length us, event | category | flops | bytes accessed | tf_op | source)
XLA Modules:
  0.0 64.7 jit_solution(18382274229480366482)
XLA Ops:
  0.6 62.8 %ensemble.1 = (f32[16,4,128]{2,1,0:T(4,128)S(1)}, bf16[2,64,8,256]{3,2,1,0:T(8,128)(2,1)S(1)}, f32[8,512]{1,0:T(8,128)S(1)}, f32[8,512]{1,0:T(8,128)S(1)}, bf16[...) custom-call(f32[16,4,128]{2,1,0:T(4,128)} %initial_hbm.1, f32[16]{0:T(128)} %rates_hbm.1, ...), custom_call_target="tpu_custom_call" | custom-call | tf_op jit(solution)/shard_map/ensemble/pallas_call | solution.py:537
  63.4 1.2 %store.1 = (f32[16,4,128]{2,1,0:T(4,128)}, bf16[64,8,512]{2,1,0:T(8,128)(2,1)}, f32[8,512]{1,0:T(8,128)}, f32[8,512]{1,0:T(8,128)}, bf16[4,128,512]{2,1,0:T(8,12...) custom-call(f32[16,4,128]{2,1,0:T(4,128)S(1)} %get-tuple-element.21.refs_0_, ...), custom_call_target="tpu_custom_call" | custom-call | tf_op jit(solution)/shard_map/store/pallas_call | solution.py:623

commit v6 on v5

--- a/solution.py
+++ b/solution.py
@@ -25,7 +25,6 @@
 F32 = jnp.float32
 BF16 = jnp.bfloat16
 
-
 def gelu_value(pre_act):
     return (
         0.5
@@ -33,13 +32,11 @@
         * (1.0 + jnp.tanh(GELU_SCALE * (pre_act + GELU_CUBE * pre_act * pre_act * pre_act)))
     )
 
-
 def gelu_slope(pre_act):
     tanh_part = jnp.tanh(GELU_SCALE * (pre_act + GELU_CUBE * pre_act * pre_act * pre_act))
     return 0.5 * (1.0 + tanh_part) + 0.5 * pre_act * (1.0 - tanh_part * tanh_part) * GELU_SCALE * (
         1.0 + 3.0 * GELU_CUBE * pre_act * pre_act
     )
-
 
 def adam_update(weight, moment, second, gradient, step_count):
     moment = BETA_ONE * moment + (1.0 - BETA_ONE) * gradient
@@ -51,12 +48,10 @@
     )
     return ((weight.astype(F32) - LEARN_RATE * update).astype(BF16), moment, second)
 
-
 def dot(left, right, left_dim, right_dim):
     return lax.dot_general(
         left, right, (((left_dim,), (right_dim,)), ((), ())), preferred_element_type=F32
     )
-
 
 def three_parts(value):
     high = value.astype(BF16)
@@ -64,7 +59,6 @@
     middle = rest.astype(BF16)
     low = (rest - middle.astype(F32)).astype(BF16)
     return high, middle, low
-
 
 def kernel(
     initial_hbm,
@@ -147,7 +141,7 @@
     at_y, at_z, at_x = me // 16, lax.rem(me // 4, 4), lax.rem(me, 4)
 
     def each(count, body):
-        width = 7 if count % 7 == 0 else 1
+        width = next(w for w in (7, 5, 3) if count % w == 0)
 
         def steps(k, carry):
             for i in range(width):
@@ -215,11 +209,25 @@
         greet(strip, group)
     greeted = 26
 
-    for load in loads[:3]:
-        load.wait()
+    loads[0].wait()
     edges[0] = initial[:, 0:2, :]
     edges[1] = initial[:, 2:4, :]
 
+    pl.semaphore_wait(barrier, greeted)
+
+    halo_copies = [
+        send(edges.at[0], halo.at[1], halo_send.at[0], halo_recv.at[1], up, g),
+        send(edges.at[1], halo.at[0], halo_send.at[1], halo_recv.at[0], down, g),
+    ]
+    for strip, group in line_peers:
+        pl.semaphore_signal(
+            plane_in_kernel,
+            inc=1,
+            device_id={"strip": strip, "group": group},
+            device_id_type=MESH,
+        )
+    for load in loads[1:3]:
+        load.wait()
     kind_row = lax.broadcasted_iota(jnp.int32, (128, 128), 0)
     field_row = 16 * (kind_row // 32) + lax.rem(kind_row, 16)
     kind_lane = lax.broadcasted_iota(jnp.int32, (64, 128), 1)
@@ -234,6 +242,14 @@
     for turn in range(ADAM):
         hits = (batch_ids[turn : turn + 1, :] == field_row).astype(F32).astype(BF16)
         counts[0, turn] = dot(ones, hits, 1, 1) * time_fits
+
+    count_copies = [
+        send(counts.at[0], counts.at[1 + i], count_send.at[i], count_recv.at[i], me, group)
+        for i, group in enumerate((far, mate, far_mate))
+    ]
+
+    for load in loads[6:]:
+        load.wait()
 
     for load in loads[3:6]:
         load.wait()
@@ -252,26 +268,6 @@
     hidden = gelu_value(pre_act).astype(BF16)
     hidden_all[0] = hidden.reshape(strips, 8, 128)
 
-    pl.semaphore_wait(barrier, greeted)
-
-    halo_copies = [
-        send(edges.at[0], halo.at[1], halo_send.at[0], halo_recv.at[1], up, g),
-        send(edges.at[1], halo.at[0], halo_send.at[1], halo_recv.at[0], down, g),
-    ]
-    count_copies = [
-        send(counts.at[0], counts.at[1 + i], count_send.at[i], count_recv.at[i], me, group)
-        for i, group in enumerate((far, mate, far_mate))
-    ]
-
-    for load in loads[6:]:
-        load.wait()
-    for strip, group in line_peers:
-        pl.semaphore_signal(
-            plane_in_kernel,
-            inc=1,
-            device_id={"strip": strip, "group": group},
-            device_id_type=MESH,
-        )
     old_weight = out_weight[...].reshape(hidden_width, 512)
     predict = dot(hidden, old_weight, 0, 0)
     own_pre = dot(in_weight[me], code, 1, 1)
@@ -465,7 +461,6 @@
             source = target = in_weight_new.at[core, me]
             several = in_weight_new.at[core, most]
             send_sem, recv_sem = row_send, row_recv
-
 
         def send_rows(k):
             t = other(k)
@@ -498,7 +493,6 @@
     own_all.wait_send()
     far_all.wait_send()
 
-
 def store(*refs):
     sources, targets, sem = refs[:7], refs[7:14], refs[14]
     width = sources[1].shape[-1]
@@ -511,7 +505,6 @@
         copy.start()
     for copy in copies:
         copy.wait()
-
 
 def shards(
     initial,
@@ -642,7 +635,6 @@
         out_v,
     )
 
-
 def solution(mesh):
     in_specs = (
         P("group", "strip", None),

time: 64.8 us -> 64.4 us (level)
  no operation moved by 1% of the time
where the time goes in v6:
time: 64.4 us; the launch traced here: 64.3 us
  Pallas kernels  63.7 us (99%)
  between operations  0.65 us (1%)
    pallas_call x1, Pallas kernels, shards(): pl.pallas_call(kernel, out_shape=(pltpu.VMEM(initial.shape, F32), pltpu.V...  62.5 us

profile of v6, /device:TPU:1, one launch (start us, length us, event | category | flops | bytes accessed | tf_op | source)
XLA Modules:
  0.0 64.3 jit_solution(10184994620990946661)
XLA Ops:
  0.6 62.5 %ensemble.1 = (f32[16,4,128]{2,1,0:T(4,128)S(1)}, bf16[2,64,8,256]{3,2,1,0:T(8,128)(2,1)S(1)}, f32[8,512]{1,0:T(8,128)S(1)}, f32[8,512]{1,0:T(8,128)S(1)}, bf16[...) custom-call(f32[16,4,128]{2,1,0:T(4,128)} %initial_hbm.1, f32[16]{0:T(128)} %rates_hbm.1, ...), custom_call_target="tpu_custom_call" | custom-call | tf_op jit(solution)/shard_map/ensemble/pallas_call | solution.py:530
  63.1 1.2 %store.1 = (f32[16,4,128]{2,1,0:T(4,128)}, bf16[64,8,512]{2,1,0:T(8,128)(2,1)}, f32[8,512]{1,0:T(8,128)}, f32[8,512]{1,0:T(8,128)}, bf16[4,128,512]{2,1,0:T(8,12...) custom-call(f32[16,4,128]{2,1,0:T(4,128)S(1)} %get-tuple-element.21.refs_0_, ...), custom_call_target="tpu_custom_call" | custom-call | tf_op jit(solution)/shard_map/store/pallas_call | solution.py:616

commit v7 on v6

--- a/solution.py
+++ b/solution.py
@@ -141,7 +141,7 @@
     at_y, at_z, at_x = me // 16, lax.rem(me // 4, 4), lax.rem(me, 4)
 
     def each(count, body):
-        width = next(w for w in (7, 5, 3) if count % w == 0)
+        width = next(w for w in (21, 15, 3) if count % w == 0)
 
         def steps(k, carry):
             for i in range(width):

time: 64.4 us -> 64.3 us (level)
  no operation moved by 1% of the time
where the time goes in v7:
time: 64.3 us; the launch traced here: 64.2 us
  Pallas kernels  63.6 us (99%)
  between operations  0.65 us (1%)
    pallas_call x1, Pallas kernels, shards(): pl.pallas_call(kernel, out_shape=(pltpu.VMEM(initial.shape, F32), pltpu.V...  62.4 us

profile of v7, /device:TPU:1, one launch (start us, length us, event | category | flops | bytes accessed | tf_op | source)
XLA Modules:
  0.0 64.2 jit_solution(16410989844273958165)
XLA Ops:
  0.6 62.4 %ensemble.1 = (f32[16,4,128]{2,1,0:T(4,128)S(1)}, bf16[2,64,8,256]{3,2,1,0:T(8,128)(2,1)S(1)}, f32[8,512]{1,0:T(8,128)S(1)}, f32[8,512]{1,0:T(8,128)S(1)}, bf16[...) custom-call(f32[16,4,128]{2,1,0:T(4,128)} %initial_hbm.1, f32[16]{0:T(128)} %rates_hbm.1, ...), custom_call_target="tpu_custom_call" | custom-call | tf_op jit(solution)/shard_map/ensemble/pallas_call | solution.py:530
  63.0 1.2 %store.1 = (f32[16,4,128]{2,1,0:T(4,128)}, bf16[64,8,512]{2,1,0:T(8,128)(2,1)}, f32[8,512]{1,0:T(8,128)}, f32[8,512]{1,0:T(8,128)}, bf16[4,128,512]{2,1,0:T(8,12...) custom-call(f32[16,4,128]{2,1,0:T(4,128)S(1)} %get-tuple-element.21.refs_0_, ...), custom_call_target="tpu_custom_call" | custom-call | tf_op jit(solution)/shard_map/store/pallas_call | solution.py:616
